TPU v7x, 128 devices: a whole 4x4x4 slice. The times are simulated.
128 devices in a mesh: gx: 8 (over z, x_lo), gy: 16 (over y, x_hi, core).
Axes of the slice: x: 4 (x_hi: 2, x_lo: 2; x = x_hi * 2 + x_lo), y: 4, z: 4, core: 2. Of those that a mesh axis runs over, the one named last changes fastest.
Arguments:
- increments: float32 [2, 3, 384, 2048], P(None, None, 'gy', 'gx'), may hold values from -6 to 6
- diffusivity: float32 [3, 384, 2048], P(None, 'gy', 'gx'), may hold values from 0.02 to 0.24
- sea_mask: int32 [384, 2048], P('gy', 'gx'), may hold values 0 or 1
- source_cells: int32 [128, 128, 3, 8, 128], P(('gx', 'gy')), may hold values from 0 to 255, as said below
- source_weights: float32 [128, 128, 8, 128], P(('gx', 'gy')), may hold values from 0.1 to 1
- source_counts: int32 [128, 128, 128], P(('gx', 'gy')), may hold values from 0 to 8
- slot_owner: int32 [128, 128, 128], P(('gx', 'gy')), may hold values from 0 to 4095
Outputs:
- smoothed: float32 [2, 3, 384, 2048], P(None, None, 'gy', 'gx')
- obs_equiv: float32 [524288], P(('gx', 'gy'))
Inputs may be any that keep to these rules, and one draw needn't show every extreme that they name: `source_cells`: component 0 is a layer below 6, component 1 a row below 24, component 2 a column below 256, all within the grid device's own tile. `source_counts`: number of leading valid entries of the slot; 0 leaves the slot empty. `slot_owner`: an observation index local to the owner.
All inputs are finite; a program needn't handle non-finite values. No bound on the sum of `sea_mask` on one device may be relied on, other than what follows from the above.
Results may differ from a plain program's by a relative error of at most 0.00002.
Values sent between devices are 32-bit elements; how exact they have to be, the bound alone decides.
No kernel may reach another device: no remote copies, remote signals or barrier semaphores. Data moves between devices by JAX's collectives and lax.ppermute only.
A program may use at most 64 MiB of HBM per device.

v0:
```python
import jax
import jax.numpy as jnp
from jax import lax
from jax.sharding import PartitionSpec as P

ITERS = 10
OBS_DEV = 4096


def padded(shard, sides, width):
    for axis, dim in sides:
        size, length = (lax.axis_size(axis), shard.shape[dim])
        up = [(i, (i + 1) % size) for i in range(size)]
        down = [(j, i) for i, j in up]
        last = lax.slice_in_dim(shard, length - width, length, axis=dim)
        first = lax.slice_in_dim(shard, 0, width, axis=dim)
        before = lax.ppermute(last, axis, up)
        after = lax.ppermute(first, axis, down)
        shard = jnp.concatenate([before, shard, after], axis=dim)
    return shard


def column_widen(array):
    wider = padded(array, ((("gx", "gy"), 1),), 1)
    return jnp.pad(wider, ((0, 0), (0, 0), (1, 1)))


def coefficient_set(diffuse_wide, wet_wide):
    centre_k = diffuse_wide[:, 1:-1, 1:-1]
    centre_w = wet_wide[1:-1, 1:-1]
    up_first = 0.5 * (centre_k + diffuse_wide[:, 2:, 1:-1]) * centre_w * wet_wide[2:, 1:-1]
    down_first = 0.5 * (centre_k + diffuse_wide[:, :-2, 1:-1]) * centre_w * wet_wide[:-2, 1:-1]
    up_second = 0.5 * (centre_k + diffuse_wide[:, 1:-1, 2:]) * centre_w * wet_wide[1:-1, 2:]
    down_second = 0.5 * (centre_k + diffuse_wide[:, 1:-1, :-2]) * centre_w * wet_wide[1:-1, :-2]
    return (up_first, down_first, up_second, down_second)


def relax(wide, coeffs, nfields, nlevels):
    span_a = wide.shape[1] - 2
    span_b = wide.shape[2] - 2
    grid = wide.reshape(nfields, nlevels, span_a + 2, span_b + 2)
    up_first, down_first, up_second, down_second = coeffs
    centre = grid[:, :, 1:-1, 1:-1]
    first_part = up_first * (grid[:, :, 2:, 1:-1] - centre) - down_first * (
        centre - grid[:, :, :-2, 1:-1]
    )
    second_part = up_second * (grid[:, :, 1:-1, 2:] - centre) - down_second * (
        centre - grid[:, :, 1:-1, :-2]
    )
    updated = centre + second_part + first_part
    return updated.reshape(nfields * nlevels, span_a, span_b)


def local(
    increments, diffusivity, sea_mask, source_cells, source_weights, source_counts, slot_owner
):
    nfields, nlevels, tile_rows, tile_cols = increments.shape
    layers = nfields * nlevels
    wet = sea_mask.astype(jnp.float32)
    started = (increments * wet).reshape(layers, tile_rows, tile_cols)
    stacked = jnp.concatenate([started, diffusivity, wet[None]], axis=0)
    moved = lax.all_to_all(stacked, "gy", split_axis=2, concat_axis=1, tiled=True)
    moved = jnp.transpose(moved, (0, 2, 1))
    field = moved[:layers]
    outer = column_widen(moved[layers:])
    coeffs = coefficient_set(outer[:nlevels], outer[nlevels])

    def advance(turn_index, flat_field):
        return relax(column_widen(flat_field), coeffs, nfields, nlevels)

    field = lax.fori_loop(0, ITERS, advance, field)
    field = lax.all_to_all(
        jnp.transpose(field, (0, 2, 1)), "gy", split_axis=1, concat_axis=2, tiled=True
    )
    smoothed = field.reshape(nfields, nlevels, tile_rows, tile_cols)
    flat_tile = smoothed.reshape(-1)
    cells_here = source_cells[0]
    flat_index = (cells_here[:, 0] * tile_rows + cells_here[:, 1]) * tile_cols + cells_here[:, 2]
    values = flat_tile[flat_index]
    valid = lax.broadcasted_iota(jnp.int32, flat_index.shape, 1) < source_counts[0][:, None, :]
    partial_value = jnp.sum(jnp.where(valid, source_weights[0] * values, jnp.float32(0.0)), axis=1)
    received = lax.all_to_all(partial_value, ("gx", "gy"), split_axis=0, concat_axis=0, tiled=True)
    obs_equiv = (
        jnp.zeros((OBS_DEV,), jnp.float32).at[slot_owner[0].reshape(-1)].add(received.reshape(-1))
    )
    return (smoothed, obs_equiv)


def solution(mesh):
    return jax.shard_map(
        local,
        mesh=mesh,
        in_specs=(
            P(None, None, "gy", "gx"),
            P(None, "gy", "gx"),
            P("gy", "gx"),
            P(("gx", "gy"), None, None, None, None),
            P(("gx", "gy"), None, None, None),
            P(("gx", "gy"), None, None),
            P(("gx", "gy"), None, None),
        ),
        out_specs=(P(None, None, "gy", "gx"), P(("gx", "gy"))),
        check_vma=False,
    )
```

profile of v0, /device:TPU:1, one launch (start us, length us, event | category | flops | bytes accessed | tf_op | source)
XLA Modules:
  0.0 976.3 jit_solution(12495031608629252336)
XLA Ops:
  3.2 1.3 copy.21
  5.4 16.8 %all_to_all.42 = f32[16,1,3840]{2,1,0:T(1,128)S(1)} all-to-all(f32[16,1,3840]{2,1,0:T(1,128)S(1)} %reshape.139), channel_id=1, replica_groups=mesh['gx'=8,'gy'=16] {'gy'}, dimensions={0} | all-to-all | bytes 491520 | tf_op jit(solution)/shard_map/all_to_all | solution.py:62
  22.8 1.3 reduce
  26.3 1.2 collective-permute-start.2
  28.3 3.8 collective-permute-done.3
  32.4 94.8 %while.12 = (s32[]{:T(128)}, f32[6,16,384]{2,1,0:T(8,128)S(1)}, f32[3,16,384]{2,1,0:T(8,128)S(1)}, f32[3,16,384]{2,1,0:T(8,128)S(1)}, f32[3,16,384]{2,1,0:T(8,128)S(1)}, /*index=5*/f32[3,16,384]{2,1,0:T(8,128)S(1)}, s32[]{:T(128)}) while((s32[]{:T(128)}, f32[6,16,384]{2,1,0:T(8,128)S(1)}, f32[3,16,384]{2,1,0:T(8,128)S(1)}, ...), condition=%wide.region_1.2_spmd, body=%wide.region_0.1_spmd.sunk | while | flops 775874 | bytes 1623037 | solution.py:71
  32.5 3.8 collective-permute-start
  37.1 6.9 collective-permute-done.1
  44.5 7.9 collective-permute-start
  54.1 7.5 collective-permute-start
  63.2 7.5 collective-permute-start
  72.4 7.5 collective-permute-start
  81.5 7.5 collective-permute-start
  90.7 7.5 collective-permute-start
  99.8 7.5 collective-permute-start
  108.9 7.5 collective-permute-start
  118.1 7.5 collective-permute-start
  127.9 1.2 reshape.141
  129.1 10.7 %all-to-all-start.1 = ((f32[16,1,2304]{2,1,0:T(1,128)}), f32[16,1,2304]{2,1,0:T(1,128)S(1)}, u32[]{:S(2)}, u32[]{:S(2)}) async-start(f32[16,1,2304]{2,1,0:T(1,128)} %reshape.141), calls=%async_computation.1 | async-start | bytes 294912 | tf_op jit(solution)/shard_map/all_to_all | solution.py:72
  140.1 7.6 all-to-all-done.1
  150.5 724.9 %gather_fusion = f32[131072]{0:T(1024)S(1)} fusion(f32[36864]{0:T(1024)S(1)} %reshape_reshape.3, s32[131072]{0:T(1024)S(1)} %fusion.10), kind=kCustom, calls=%fused_computation | custom fusion | bytes 1572864 | tf_op jit(solution)/shard_map/gather | solution.py:79
  876.3 4.1 all-to-all-start.2
  881.5 8.3 all-to-all-done.2
  889.9 86.4 %scatter_custom_fusion = f32[4096]{0:T(1024)} fusion(s32[16384]{0:T(1024)S(1)} %bitcast.73, f32[16384]{0:T(1024)S(1)} %bitcast.72, f32[]{:T(128)} %constant.27.clone.1), kind=kCustom, calls=%fused_computation.56 | custom fusion | flops 16384 | bytes 16388 | tf_op jit(solution)/shard_map/scatter-add | solution.py:84
  (98 shorter events, 28.8 us)
Async XLA Ops:
  26.3 2.0 collective-permute-start.2
  27.5 4.6 collective-permute-start.3
  32.5 4.7 collective-permute-start
  36.2 7.8 collective-permute-start.1
  44.5 8.7 collective-permute-start
  52.4 1.2 collective-permute-start.1
  54.1 8.3 collective-permute-start
  61.6 1.2 collective-permute-start.1
  63.2 8.3 collective-permute-start
  70.7 1.2 collective-permute-start.1
  72.4 8.3 collective-permute-start
  79.9 1.2 collective-permute-start.1
  81.5 8.3 collective-permute-start
  89.0 1.2 collective-permute-start.1
  90.7 8.3 collective-permute-start
  98.1 1.2 collective-permute-start.1
  99.8 8.3 collective-permute-start
  107.3 1.2 collective-permute-start.1
  108.9 8.3 collective-permute-start
  116.4 1.2 collective-permute-start.1
  118.1 8.3 collective-permute-start
  125.6 1.2 collective-permute-start.1
  129.1 18.6 %all-to-all-start.1 = ((f32[16,1,2304]{2,1,0:T(1,128)}), f32[16,1,2304]{2,1,0:T(1,128)S(1)}, u32[]{:S(2)}, u32[]{:S(2)}) async-start(f32[16,1,2304]{2,1,0:T(1,128)} %reshape.141), calls=%async_computation.1 | async-start | bytes 294912 | tf_op jit(solution)/shard_map/all_to_all | solution.py:72
  876.3 13.6 %all-to-all-start.2 = ((f32[128,1,128]{2,1,0:T(1,128)}), f32[128,1,128]{2,1,0:T(1,128)S(1)}, u32[]{:S(2)}, u32[]{:S(2)}) async-start(f32[128,1,128]{2,1,0:T(1,128)} %bitcast.20), calls=%async_computation.2 | async-start | bytes 131072 | tf_op jit(solution)/shard_map/all_to_all | solution.py:82
  (6 other events, 2921.9 us)
where the time goes:
time: 977 us; the launch traced here: 976 us
  local copies, waits for them, and re-layouts  735 us (75%)
  other arithmetic  96.9 us (10%)
  starting transfers between devices  87.7 us (9%)
  waiting for transfers between devices  38.8 us (4%)
  blocking collectives  16.8 us (2%)
    gather x1, local copies, waits for them, and re-layouts, local(): values = flat_tile[flat_index]  725 us
    scatter-add x1, other arithmetic, local(): jnp.zeros((OBS_DEV,), jnp.float32).at[slot_owner[0].reshape(-1)]  86.4 us
    ppermute x11, starting transfers between devices, padded(): after = lax.ppermute(first, axis, down)  71.7 us
  transfers between devices with their start and end apart: 24, of which 24 were waited for; matrix products, arithmetic and copies ran while one was open for 0% of the time, Pallas kernels for 0%

commit v1 on v0

v1 whole, which is shorter than its diff:
```python
import jax
import jax.numpy as jnp
from jax import lax
from jax.experimental import pallas as pl
from jax.experimental.pallas import tpu as pltpu
from jax.sharding import PartitionSpec as P

F32 = jnp.float32
BF16 = jnp.bfloat16
ITERS = 10
HALO = 10
OBS_DEV = 4096
LAYERS = 6
LEVELS = 3
ARRAYS = LAYERS + LEVELS
CY = 24
CX = 256
LANES = 128
STRIDE = 14
ROWS = 48
COLS = 384
TABLE = LAYERS * CY * 2
TURN = 8
OWNERS = 128
BLOCK = 32


def iota(shape, dim):
    return lax.broadcasted_iota(jnp.int32, shape, dim)


def pack_kernel(inc_ref, dif_ref, mask_ref, base_ref, first_ref, last_ref):
    wet = mask_ref[...].astype(F32)
    lane = iota((CY, LANES), 1)
    first = jnp.zeros((CY, LANES), F32)
    last = jnp.zeros((CY, LANES), F32)
    for a in range(ARRAYS):
        values = (inc_ref[a] if a < LAYERS else dif_ref[a - LAYERS]) * wet
        base_ref[a] = values
        mine = (lane >= STRIDE * a) & (lane < STRIDE * a + HALO)
        left = values[:, :LANES]
        right = values[:, LANES:]
        if a:
            left = pltpu.roll(left, STRIDE * a, 1)
        right = pltpu.roll(right, STRIDE * a + HALO, 1)
        first = jnp.where(mine, left, first)
        last = jnp.where(mine, right, last)
    first_ref[...] = first
    last_ref[...] = last


def rows_kernel(base_ref, east_ref, west_ref, low_ref, high_ref):
    for a in range(ARRAYS + 1):
        for ref, start in ((low_ref, 0), (high_ref, CY - HALO)):
            if a < ARRAYS:
                ref[pl.ds(HALO * a, HALO), :] = base_ref[a, pl.ds(start, HALO), :]
            else:
                ref[pl.ds(HALO * a, HALO), pl.ds(0, LANES)] = east_ref[pl.ds(start, HALO), :]
                ref[pl.ds(HALO * a, HALO), pl.ds(LANES, LANES)] = west_ref[pl.ds(start, HALO), :]


def smooth(base_ref, east_ref, west_ref, north_ref, south_ref, wide_ref, across_ref, up_ref, out_ref):
    lane_tile = iota((CY, LANES), 1)
    lane_rows = iota((HALO, LANES), 1)

    def side(east, west, a, lane):
        if a:
            east = pltpu.roll(east, LANES - STRIDE * a, 1)
        west = pltpu.roll(west, (LANES - HALO - STRIDE * a) % LANES, 1)
        halo = jnp.where(lane < HALO, east, 0.0)
        return jnp.where(lane >= LANES - HALO, west, halo)

    strip = pl.ds(HALO * ARRAYS, HALO)
    for a in range(ARRAYS):
        wide_ref[a, pl.ds(0, CY), pl.ds(0, CX)] = base_ref[a]
        wide_ref[a, pl.ds(0, CY), pl.ds(CX, LANES)] = side(east_ref[...], west_ref[...], a, lane_tile)
        wide_ref[a, pl.ds(CY, CY), :] = jnp.zeros((CY, COLS), F32)
        for ref, start in ((north_ref, CY), (south_ref, ROWS - HALO)):
            wide_ref[a, pl.ds(start, HALO), pl.ds(0, CX)] = ref[pl.ds(HALO * a, HALO), :]
            wide_ref[a, pl.ds(start, HALO), pl.ds(CX, LANES)] = side(
                ref[strip, pl.ds(0, LANES)], ref[strip, pl.ds(LANES, LANES)], a, lane_rows
            )
    for level in range(LEVELS):
        here = wide_ref[LAYERS + level]
        for ref, axis, size in ((across_ref, 1, COLS), (up_ref, 0, ROWS)):
            there = pltpu.roll(here, size - 1, axis)
            both = (here > 0.0) & (there > 0.0)
            ref[level] = jnp.where(both, 0.5 * (here + there), 0.0)

    def one_layer(layer, _):
        level = layer % LEVELS

        def turn(_, field):
            east = across_ref[level] * (pltpu.roll(field, COLS - 1, 1) - field)
            north = up_ref[level] * (pltpu.roll(field, ROWS - 1, 0) - field)
            return field + (east - pltpu.roll(east, 1, 1)) + (north - pltpu.roll(north, 1, 0))

        field = lax.fori_loop(0, ITERS, turn, wide_ref[layer])
        out_ref[layer] = field[:CY, :CX]
        return 0

    lax.fori_loop(0, LAYERS, one_layer, 0)


def choose(parts, bits):
    turn = 0
    while len(parts) > 1:
        pairs = [
            jnp.where(bits[turn], parts[2 * j + 1], parts[2 * j]) for j in range(len(parts) // 2)
        ]
        parts = pairs + parts[2 * len(pairs):]
        turn += 1
    return parts[0]


def main_kernel(
    base_ref, east_ref, west_ref, north_ref, south_ref, cells_ref, weights_ref, counts_ref,
    smooth_ref, partial_ref, wide_ref, across_ref, up_ref, table_ref,
):
    @pl.when(pl.program_id(0) == 0)
    def _():
        smooth(
            base_ref, east_ref, west_ref, north_ref, south_ref, wide_ref, across_ref, up_ref,
            smooth_ref,
        )
        for half in range(2):
            for layer in range(LAYERS):
                values = smooth_ref[layer, :, pl.ds(half * LANES, LANES)]
                coarse = values.astype(BF16)
                fine = (values - coarse.astype(F32)).astype(BF16)
                rows = pl.ds((half * LAYERS + layer) * CY, CY)
                table_ref[rows, pl.ds(0, LANES)] = coarse.astype(F32)
                table_ref[rows, pl.ds(LANES, LANES)] = fine.astype(F32)

    table = table_ref[...].astype(BF16)
    lane_id = iota((LANES, LANES), 0).astype(BF16)
    sub_id = iota((8, LANES), 0)

    def one_owner(o):
        layer = cells_ref[o, 0]
        row = cells_ref[o, 1]
        col = cells_ref[o, 2]
        rows_at = (col >> 7) * (LAYERS * CY) + layer * CY + row
        lane_at = (col & (LANES - 1)).astype(F32).astype(BF16)
        weights = jnp.where(sub_id < counts_ref[pl.ds(o, 1), :], weights_ref[o], 0.0)
        total = jnp.zeros((8, LANES), F32)
        for k in range(0, 8, 2):
            picks = []
            for j in (k, k + 1):
                lane_row = jnp.broadcast_to(lane_at[j:j + 1, :], (LANES, LANES))
                picks.append(jnp.where(lane_id == lane_row, BF16(1), BF16(0)))
            pick = jnp.concatenate(picks, axis=1)
            found = jnp.dot(
                table, jnp.concatenate([pick, pick], axis=0), preferred_element_type=F32
            )
            for j in (0, 1):
                block = found[:, j * LANES:(j + 1) * LANES]
                at = jnp.broadcast_to(rows_at[k + j:k + j + 1, :], (8, LANES))
                bits = [(at & (8 << b)) != 0 for b in range(6)]
                value = choose([block[8 * q:8 * q + 8] for q in range(TABLE // 8)], bits)
                value = jnp.where(sub_id == (at & 7), value, 0.0)
                total = total + value * jnp.broadcast_to(weights[k + j:k + j + 1, :], (8, LANES))
        partial_ref[o] = jnp.sum(total, axis=0, keepdims=True)

    def some(i, _):
        for j in range(TURN):
            one_owner(i * TURN + j)
        return 0

    lax.fori_loop(0, BLOCK // TURN, some, 0)


def owner_kernel(values_ref, slots_ref, out_ref):
    high_id = iota((32, LANES), 0)
    low_id = iota((LANES, LANES), 0)
    total = jnp.zeros((64, LANES), F32)
    for g in range(0, OWNERS, 8):
        left = []
        right = []
        for j in range(g, g + 8):
            value = values_ref[j]
            slot = slots_ref[pl.ds(j, 1), :]
            coarse = value.astype(BF16).astype(F32)
            fine = value - coarse
            high = high_id == (slot >> 7)
            left.append(
                jnp.concatenate([jnp.where(high, coarse, 0.0), jnp.where(high, fine, 0.0)], axis=0)
            )
            right.append(jnp.where(low_id == (slot & 127), 1.0, 0.0))
        total = total + lax.dot_general(
            jnp.concatenate(left, axis=1).astype(BF16),
            jnp.concatenate(right, axis=1).astype(BF16),
            (((1,), (1,)), ((), ())),
            preferred_element_type=F32,
        )
    out_ref[...] = total[:32] + total[32:]


def shape(*dims):
    return jax.ShapeDtypeStruct(dims, F32)


def shift(array, axis, step, wrap):
    size = lax.axis_size(axis)
    pairs = [(i, (i + step) % size) for i in range(size) if wrap or 0 <= i + step < size]
    return lax.ppermute(array, axis, pairs)


def whole(*dims):
    return pl.BlockSpec(dims, lambda i: (0,) * len(dims))


def local(
    increments, diffusivity, sea_mask, source_cells, source_weights, source_counts, slot_owner
):
    base, first, last = pl.pallas_call(
        pack_kernel,
        out_shape=(shape(ARRAYS, CY, CX), shape(CY, LANES), shape(CY, LANES)),
        name="pack",
    )(increments.reshape(LAYERS, CY, CX), diffusivity, sea_mask)
    east = shift(first, "gx", -1, True)
    west = shift(last, "gx", 1, True)
    low, high = pl.pallas_call(
        rows_kernel,
        out_shape=(shape(HALO * (ARRAYS + 1), CX), shape(HALO * (ARRAYS + 1), CX)),
        name="rows",
    )(base, east, west)
    north = shift(low, "gy", -1, False)
    south = shift(high, "gy", 1, False)
    strip = (HALO * (ARRAYS + 1), CX)
    smoothed, partial_value = pl.pallas_call(
        main_kernel,
        grid=(OWNERS // BLOCK,),
        in_specs=[
            whole(ARRAYS, CY, CX),
            whole(CY, LANES),
            whole(CY, LANES),
            whole(*strip),
            whole(*strip),
            pl.BlockSpec((BLOCK, 3, 8, LANES), lambda i: (i, 0, 0, 0)),
            pl.BlockSpec((BLOCK, 8, LANES), lambda i: (i, 0, 0)),
            pl.BlockSpec((BLOCK, LANES), lambda i: (i, 0)),
        ],
        out_specs=(whole(LAYERS, CY, CX), pl.BlockSpec((BLOCK, 1, LANES), lambda i: (i, 0, 0))),
        out_shape=(shape(LAYERS, CY, CX), shape(OWNERS, 1, LANES)),
        scratch_shapes=[
            pltpu.VMEM((ARRAYS, ROWS, COLS), F32),
            pltpu.VMEM((LEVELS, ROWS, COLS), F32),
            pltpu.VMEM((LEVELS, ROWS, COLS), F32),
            pltpu.VMEM((TABLE, 2 * LANES), F32),
        ],
        name="main",
    )(base, east, west, north, south, source_cells[0], source_weights[0], source_counts[0])
    received = lax.all_to_all(
        partial_value, ("gx", "gy"), split_axis=0, concat_axis=0, tiled=True
    )
    obs_equiv = pl.pallas_call(
        owner_kernel, out_shape=shape(OBS_DEV // LANES, LANES), name="owner"
    )(received, slot_owner[0])
    return smoothed.reshape(increments.shape), obs_equiv.reshape(-1)


def solution(mesh):
    return jax.shard_map(
        local,
        mesh=mesh,
        in_specs=(
            P(None, None, "gy", "gx"),
            P(None, "gy", "gx"),
            P("gy", "gx"),
            P(("gx", "gy"), None, None, None, None),
            P(("gx", "gy"), None, None, None),
            P(("gx", "gy"), None, None),
            P(("gx", "gy"), None, None),
        ),
        out_specs=(P(None, None, "gy", "gx"), P(("gx", "gy"))),
        check_vma=False,
    )
```

time: 977 us -> 82 us (0.08)
  local copies, waits for them, and re-layouts: 735 us -> 1.23 us
  other arithmetic: 96.9 us -> 0 us
  starting transfers between devices: 87.7 us -> 13.8 us
  Pallas kernels: 0 us -> 41.7 us
  waiting for transfers between devices: 38.8 us -> 6.87 us
    gather x1 -> x0, local copies, waits for them, and re-layouts: 725 us -> none  [local(): values = flat_tile[flat_index]]
    scatter-add x1 -> x0, other arithmetic: 86.4 us -> none  [local(): jnp.zeros((OBS_DEV,), jnp.float32).at[slot_owner[0].reshape(-1)]]
    ppermute x22 -> x4, starting transfers between devices: 72.9 us -> 13.8 us  [shift(): return lax.ppermute(array, axis, pairs)]
    pallas_call x0 -> x4, Pallas kernels: none -> 41.7 us  [the longest x1 35.3 us: local(): pl.pallas_call(main_kernel, grid=(OWNERS // BLOCK,), in_specs=[whole(ARRA...]
    ppermute x22 -> x4, waiting for transfers between devices: 22.9 us -> 6.87 us  [shift(): return lax.ppermute(array, axis, pairs)]
    all_to_all x2 -> x0, waiting for transfers between devices: 16 us -> none  [the longest x1 8.32 us: local(): lax.all_to_all(partial_value, ('gx', 'gy'), split_axis=0, concat_axis=0,...]
    all_to_all x2 -> x0, starting transfers between devices: 14.8 us -> none  [the longest x1 10.7 us: local(): lax.all_to_all(jnp.transpose(field, (0, 2, 1)), 'gy', split_axis=1, conca...]
  transfers between devices with their start and end apart: 24 -> 4, of which waited for: 24 -> 4; matrix products, arithmetic and copies ran while one was open for 0% -> 0% of each run, Pallas kernels for 0% -> 0%
where the time goes in v1:
time: 82 us; the launch traced here: 81.8 us
  Pallas kernels  41.7 us (51%)
  blocking collectives  17.6 us (21%)
  starting transfers between devices  13.8 us (17%)
  waiting for transfers between devices  6.87 us (8%)
  local copies, waits for them, and re-layouts  1.23 us (2%)
    pallas_call x1, Pallas kernels, local(): pl.pallas_call(main_kernel, grid=(OWNERS // BLOCK,), in_specs=[whole(ARRA...  35.3 us
    all_to_all x1, blocking collectives, local(): lax.all_to_all(partial_value, ('gx', 'gy'), split_axis=0, concat_axis=0,...  17.6 us
    ppermute x4, starting transfers between devices, shift(): return lax.ppermute(array, axis, pairs)  13.8 us
    ppermute x4, waiting for transfers between devices, shift(): return lax.ppermute(array, axis, pairs)  6.87 us
    pallas_call x1, Pallas kernels, local(): pl.pallas_call(owner_kernel, out_shape=shape(OBS_DEV // LANES, LANES), na...  3.08 us
    pallas_call x1, Pallas kernels, local(): pl.pallas_call(pack_kernel, out_shape=(shape(ARRAYS, CY, CX), shape(CY, L...  1.67 us
    pallas_call x1, Pallas kernels, local(): pl.pallas_call(rows_kernel, out_shape=(shape(HALO * (ARRAYS + 1), CX), sh...  1.66 us
  transfers between devices with their start and end apart: 4, of which 4 were waited for; matrix products, arithmetic and copies ran while one was open for 0% of the time, Pallas kernels for 0%

profile of v1, /device:TPU:1, one launch (start us, length us, event | category | flops | bytes accessed | tf_op | source)
XLA Modules:
  0.0 81.8 jit_solution(9681312887911839038)
XLA Ops:
  0.6 1.7 %pack.1 = (f32[9,24,256]{2,1,0:T(8,128)}, f32[24,128]{1,0:T(8,128)}, f32[24,128]{1,0:T(8,128)}) custom-call(f32[6,24,256]{2,1,0:T(8,128)} %bitcast.9, f32[3,24,256]{2,1,0:T(8,128)} %dif_ref.1, s32[24,256]{1,0:T(8,128)} %mask_ref.1), custom_call_target="tpu_custom_call" | custom-call | tf_op jit(solution)/shard_map/pack/pallas_call | solution.py:216
  2.3 5.5 %collective-permute-start = (f32[24,128]{1,0:T(8,128)}, f32[24,128]{1,0:T(8,128)S(1)}, u32[]{:S(2)}, u32[]{:S(2)}) collective-permute-start(f32[24,128]{1,0:T(8,128)} %get-tuple-element.10), channel_id=1, source_target_pairs={{0,112},{16,0},{32,16},{48,32},{64,48},{80,64},{96,80},{112,96},{1... | collective-permute-start | bytes 36872 | tf_op jit(solution)/shard_map/ppermute | solution.py:206
  7.8 0.0 collective-permute-start.1
  7.8 1.0 %collective-permute-done.east_ref = f32[24,128]{1,0:T(8,128)S(1)} collective-permute-done((f32[24,128]{1,0:T(8,128)}, f32[24,128]{1,0:T(8,128)S(1)}, u32[]{:S(2)}, u32[]{:S(2)}) %collective-permute-start) | collective-permute-done | bytes 12320 | tf_op jit(solution)/shard_map/ppermute | solution.py:206
  8.9 0.0 copy-start.2
  8.9 3.8 %collective-permute-done.1.west_ref = f32[24,128]{1,0:T(8,128)S(1)} collective-permute-done((f32[24,128]{1,0:T(8,128)}, f32[24,128]{1,0:T(8,128)S(1)}, u32[]{:S(2)}, u32[]{:S(2)}) %collective-permute-start.1) | collective-permute-done | bytes 12320 | tf_op jit(solution)/shard_map/ppermute | solution.py:206
  12.7 0.0 copy-start.3
  12.7 0.0 copy-done.2
  12.7 0.6 copy-done.3
  13.3 1.7 %rows.1 = (f32[100,256]{1,0:T(8,128)}, f32[100,256]{1,0:T(8,128)}) custom-call(f32[9,24,256]{2,1,0:T(8,128)} %get-tuple-element.9.base_ref, f32[24,128]{1,0:T(8,128)} %copy-done.2, f32[24,128]{1,0:T(8,128)} %copy-done.3), custom_call_target="tpu_custom_call" | custom-call | tf_op jit(solution)/shard_map/rows/pallas_call | solution.py:223
  14.9 4.0 %collective-permute-start.2 = (f32[100,256]{1,0:T(8,128)}, f32[100,256]{1,0:T(8,128)S(1)}, u32[]{:S(2)}, u32[]{:S(2)}) collective-permute-start(f32[100,256]{1,0:T(8,128)} %get-tuple-element.12), channel_id=1, source_target_pairs={{1,0},{2,1},{3,2},{4,3},{5,4},{6,5},{7,6},{8,7},{9,8},{10,9},{11,1... | collective-permute-start | bytes 307208 | tf_op jit(solution)/shard_map/ppermute | solution.py:206
  18.9 4.3 %collective-permute-start.3 = (f32[100,256]{1,0:T(8,128)}, f32[100,256]{1,0:T(8,128)S(1)}, u32[]{:S(2)}, u32[]{:S(2)}) collective-permute-start(f32[100,256]{1,0:T(8,128)} %get-tuple-element.13), channel_id=1, source_target_pairs={{0,1},{1,2},{2,3},{3,4},{4,5},{5,6},{6,7},{7,8},{8,9},{9,10},{10,1... | collective-permute-start | bytes 307208 | tf_op jit(solution)/shard_map/ppermute | solution.py:206
  23.2 0.7 collective-permute-done.2.north_ref
  23.9 0.0 copy-start
  23.9 1.4 %collective-permute-done.3.south_ref = f32[100,256]{1,0:T(8,128)S(1)} collective-permute-done((f32[100,256]{1,0:T(8,128)}, f32[100,256]{1,0:T(8,128)S(1)}, u32[]{:S(2)}, u32[]{:S(2)}) %collective-permute-start.3) | collective-permute-done | bytes 102432 | tf_op jit(solution)/shard_map/ppermute | solution.py:206
  25.2 0.0 copy-start.1
  25.2 0.0 copy-done
  25.2 0.6 copy-done.1
  25.9 35.3 %main.1 = (f32[6,24,256]{2,1,0:T(8,128)}, f32[128,1,128]{2,1,0:T(1,128)}) custom-call(f32[9,24,256]{2,1,0:T(8,128)} %get-tuple-element.9.base_ref, f32[24,128]{1,0:T(8,128)} %copy-done.2, f32[24,128]{1,0:T(8,128)} %copy-done.3, f32[100,256]{1,0:T(8,128)} %copy-done, f32[100,256]{1,0:T(8,128)} %copy-done.1, s32[128,3,8,128]{3,2,1,0:T(8,128)} %bitcast.7, ...), custom_call_target="tpu_custom_call" | custom-call | tf_op jit(solution)/shard_map/main/pallas_call | solution.py:231
  61.1 17.6 %all_to_all.5.values_ref = f32[128,1,128]{2,1,0:T(1,128)} all-to-all(f32[128,1,128]{2,1,0:T(1,128)} %get-tuple-element.15), channel_id=1, replica_groups=mesh['gx'=8,'gy'=16] {'gx','gy'}, dimensions={0} | all-to-all | bytes 131072 | tf_op jit(solution)/shard_map/all_to_all | solution.py:254
  78.7 3.1 %owner.1 = f32[32,128]{1,0:T(8,128)} custom-call(f32[128,1,128]{2,1,0:T(1,128)} %all_to_all.5.values_ref, s32[128,128]{1,0:T(8,128)} %bitcast.11), custom_call_target="tpu_custom_call" | custom-call | tf_op jit(solution)/shard_map/owner/pallas_call | solution.py:257
Async XLA Ops:
  2.3 6.6 %collective-permute-start = (f32[24,128]{1,0:T(8,128)}, f32[24,128]{1,0:T(8,128)S(1)}, u32[]{:S(2)}, u32[]{:S(2)}) collective-permute-start(f32[24,128]{1,0:T(8,128)} %get-tuple-element.10), channel_id=1, source_target_pairs={{0,112},{16,0},{32,16},{48,32},{64,48},{80,64},{96,80},{112,96},{1... | collective-permute-start | bytes 36872 | tf_op jit(solution)/shard_map/ppermute | solution.py:206
  7.8 4.9 %collective-permute-start.1 = (f32[24,128]{1,0:T(8,128)}, f32[24,128]{1,0:T(8,128)S(1)}, u32[]{:S(2)}, u32[]{:S(2)}) collective-permute-start(f32[24,128]{1,0:T(8,128)} %get-tuple-element.11), channel_id=1, source_target_pairs={{0,16},{16,32},{32,48},{48,64},{64,80},{80,96},{96,112},{112,0},{1... | collective-permute-start | bytes 36872 | tf_op jit(solution)/shard_map/ppermute | solution.py:206
  8.9 3.8 %copy-start.2 = (f32[24,128]{1,0:T(8,128)}, f32[24,128]{1,0:T(8,128)S(1)}, u32[]{:S(2)}) copy-start(f32[24,128]{1,0:T(8,128)S(1)} %collective-permute-done.east_ref) | copy-start | bytes 36868
  12.7 0.6 copy-start.3
  14.9 8.9 %collective-permute-start.2 = (f32[100,256]{1,0:T(8,128)}, f32[100,256]{1,0:T(8,128)S(1)}, u32[]{:S(2)}, u32[]{:S(2)}) collective-permute-start(f32[100,256]{1,0:T(8,128)} %get-tuple-element.12), channel_id=1, source_target_pairs={{1,0},{2,1},{3,2},{4,3},{5,4},{6,5},{7,6},{8,7},{9,8},{10,9},{11,1... | collective-permute-start | bytes 307208 | tf_op jit(solution)/shard_map/ppermute | solution.py:206
  18.9 6.3 %collective-permute-start.3 = (f32[100,256]{1,0:T(8,128)}, f32[100,256]{1,0:T(8,128)S(1)}, u32[]{:S(2)}, u32[]{:S(2)}) collective-permute-start(f32[100,256]{1,0:T(8,128)} %get-tuple-element.13), channel_id=1, source_target_pairs={{0,1},{1,2},{2,3},{3,4},{4,5},{5,6},{6,7},{7,8},{8,9},{9,10},{10,1... | collective-permute-start | bytes 307208 | tf_op jit(solution)/shard_map/ppermute | solution.py:206
  23.9 1.4 %copy-start = (f32[100,256]{1,0:T(8,128)}, f32[100,256]{1,0:T(8,128)S(1)}, u32[]{:S(2)}) copy-start(f32[100,256]{1,0:T(8,128)S(1)} %collective-permute-done.2.north_ref) | copy-start | bytes 307204
  25.2 0.6 copy-start.1

commit v2 on v1

v2 whole, which is shorter than its diff:
```python
import jax
import jax.numpy as jnp
from jax import lax
from jax.experimental import pallas as pl
from jax.experimental.pallas import tpu as pltpu
from jax.sharding import PartitionSpec as P

F32 = jnp.float32
BF16 = jnp.bfloat16
ITERS = 10
HALO = 10
OBS_DEV = 4096
LAYERS = 6
LEVELS = 3
ARRAYS = LAYERS + LEVELS
CY = 24
CX = 256
LANES = 128
STRIDE = 14
ROWS = 48
WIDE = 3
TABLE = LAYERS * CY * 2
TURN = 16
LOOKED_UP = 4
BANDS = 6
UNROLL = 5
OWNERS = 128
VMEM = pl.BlockSpec(memory_space=pltpu.VMEM)


def iota(shape, dim):
    return lax.broadcasted_iota(jnp.int32, shape, dim)


def pack_kernel(inc_ref, dif_ref, mask_ref, base_ref, first_ref, last_ref):
    wet = mask_ref[...].astype(F32)
    lane = iota((CY, LANES), 1)
    first = jnp.zeros((CY, LANES), F32)
    last = jnp.zeros((CY, LANES), F32)
    for a in range(ARRAYS):
        values = (inc_ref[a] if a < LAYERS else dif_ref[a - LAYERS]) * wet
        base_ref[a] = values
        mine = (lane >= STRIDE * a) & (lane < STRIDE * a + HALO)
        left = values[:, :LANES]
        right = values[:, LANES:]
        if a:
            left = pltpu.roll(left, STRIDE * a, 1)
        right = pltpu.roll(right, STRIDE * a + HALO, 1)
        first = jnp.where(mine, left, first)
        last = jnp.where(mine, right, last)
    first_ref[...] = first
    last_ref[...] = last


def rows_kernel(base_ref, east_ref, west_ref, low_ref, high_ref):
    for a in range(ARRAYS + 1):
        for ref, start in ((low_ref, 0), (high_ref, CY - HALO)):
            if a < ARRAYS:
                ref[pl.ds(HALO * a, HALO), :] = base_ref[a, pl.ds(start, HALO), :]
            else:
                ref[pl.ds(HALO * a, HALO), pl.ds(0, LANES)] = east_ref[pl.ds(start, HALO), :]
                ref[pl.ds(HALO * a, HALO), pl.ds(LANES, LANES)] = west_ref[pl.ds(start, HALO), :]


def smooth(
    base_ref, east_ref, west_ref, north_ref, south_ref, out_ref, wide_ref, coeff_ref,
    table_ref,
):
    lane_tile = iota((CY, LANES), 1)
    lane_rows = iota((HALO, LANES), 1)

    def side(east, west, a, lane):
        if a:
            east = pltpu.roll(east, LANES - STRIDE * a, 1)
        west = pltpu.roll(west, (LANES - HALO - STRIDE * a) % LANES, 1)
        halo = jnp.where(lane < HALO, east, 0.0)
        return jnp.where(lane >= LANES - HALO, west, halo)

    strip = pl.ds(HALO * ARRAYS, HALO)
    for a in range(ARRAYS):
        for v in range(2):
            lanes = pl.ds(v * LANES, LANES)
            wide_ref[a, v, pl.ds(0, CY), :] = base_ref[a, :, lanes]
            wide_ref[a, v, pl.ds(CY, CY), :] = jnp.zeros((CY, LANES), F32)
            wide_ref[a, v, pl.ds(CY, HALO), :] = north_ref[pl.ds(HALO * a, HALO), lanes]
            wide_ref[a, v, pl.ds(ROWS - HALO, HALO), :] = south_ref[pl.ds(HALO * a, HALO), lanes]
        wide_ref[a, 2, pl.ds(0, CY), :] = side(east_ref[...], west_ref[...], a, lane_tile)
        wide_ref[a, 2, pl.ds(CY, CY), :] = jnp.zeros((CY, LANES), F32)
        for ref, start in ((north_ref, CY), (south_ref, ROWS - HALO)):
            wide_ref[a, 2, pl.ds(start, HALO), :] = side(
                ref[strip, pl.ds(0, LANES)], ref[strip, pl.ds(LANES, LANES)], a, lane_rows
            )

    lane = iota((8, LANES), 1)

    def bands(a):
        return [
            [wide_ref[a, v, pl.ds(b, 8, stride=BANDS), :] for v in range(WIDE)]
            for b in range(BANDS)
        ]

    def to_east(parts):
        turned = [pltpu.roll(part, LANES - 1, 1) for part in parts]
        return [
            jnp.where(lane == LANES - 1, turned[(v + 1) % WIDE], turned[v]) for v in range(WIDE)
        ]

    def to_west(parts):
        turned = [pltpu.roll(part, 1, 1) for part in parts]
        return [jnp.where(lane == 0, turned[(v - 1) % WIDE], turned[v]) for v in range(WIDE)]

    def to_north(values):
        return values[1:] + [[pltpu.roll(part, 7, 0) for part in values[0]]]

    def to_south(values):
        return [[pltpu.roll(part, 1, 0) for part in values[-1]]] + values[:-1]

    def face(here, there):
        return [
            jnp.where((x > 0.0) & (y > 0.0), 0.5 * (x + y), 0.0) for x, y in zip(here, there)
        ]

    for level in range(LEVELS):
        here = bands(LAYERS + level)
        north = [face(x, y) for x, y in zip(here, to_north(here))]
        south = to_south(north)
        for b in range(BANDS):
            east = face(here[b], to_east(here[b]))
            west = to_west(east)
            for v in range(WIDE):
                sides = (east[v], west[v], north[b][v], south[b][v])
                keep = 1.0 - ((sides[0] + sides[1]) + (sides[2] + sides[3]))
                for i, side_value in enumerate((keep,) + sides):
                    coeff_ref[level, i, b, v] = side_value

    def step(field, level):
        north = to_north(field)
        south = to_south(field)
        updated = []
        for b in range(BANDS):
            around = (field[b], to_east(field[b]), to_west(field[b]), north[b], south[b])
            parts = []
            for v in range(WIDE):
                terms = [coeff_ref[level, i, b, v] * near[v] for i, near in enumerate(around)]
                parts.append(terms[0] + ((terms[1] + terms[2]) + (terms[3] + terms[4])))
            updated.append(parts)
        return updated

    for level in range(LEVELS):

        def turn(_, fields):
            for _ in range(UNROLL):
                fields = [step(field, level) for field in fields]
            return fields

        pair = lax.fori_loop(0, ITERS // UNROLL, turn, [bands(level), bands(level + LEVELS)])
        for layer, field in zip((level, level + LEVELS), pair):
            for v in range(2):
                first = (v * LAYERS + layer) * CY
                for b in range(BANDS):
                    table_ref[pl.ds(first + b, CY // BANDS, stride=BANDS), :] = field[b][v][
                        :CY // BANDS
                    ]
                out_ref[layer, :, pl.ds(v * LANES, LANES)] = table_ref[pl.ds(first, CY), :]


def choose(parts, bits):
    turn = 0
    while len(parts) > 1:
        pairs = [
            jnp.where(bits[turn], parts[2 * j + 1], parts[2 * j]) for j in range(len(parts) // 2)
        ]
        parts = pairs + parts[2 * len(pairs):]
        turn += 1
    return parts[0]


def main_kernel(
    base_ref, east_ref, west_ref, north_ref, south_ref, cells_far, weights_far, counts_far,
    smooth_ref, partial_ref, wide_ref, coeff_ref, table_ref, split_ref, cells_ref, weights_ref,
    counts_ref, arrived,
):
    fetches = [
        pltpu.make_async_copy(far, ref, arrived.at[i])
        for i, (far, ref) in enumerate(
            ((cells_far, cells_ref), (weights_far, weights_ref), (counts_far, counts_ref))
        )
    ]
    for fetch in fetches:
        fetch.start()
    smooth(
        base_ref, east_ref, west_ref, north_ref, south_ref, smooth_ref, wide_ref, coeff_ref,
        table_ref,
    )
    values = table_ref[...]
    coarse = values.astype(BF16)
    split_ref[:, pl.ds(0, LANES)] = coarse
    split_ref[:, pl.ds(LANES, LANES)] = (values - coarse.astype(F32)).astype(BF16)

    for fetch in fetches:
        fetch.wait()
    split = split_ref[...]
    lane_id = iota((LANES, LANES), 0).astype(BF16)
    sub_id = iota((8, LANES), 0)

    def places(o):
        col = cells_ref[o, 2]
        rows_at = (col >> 7) * (LAYERS * CY) + cells_ref[o, 0] * CY + cells_ref[o, 1]
        weights = jnp.where(sub_id < counts_ref[pl.ds(o, 1), :], weights_ref[o], 0.0)
        return rows_at, col & (LANES - 1), weights

    def by_matmul(o):
        rows_at, lane_at, weights = places(o)
        lane_at = lane_at.astype(F32).astype(BF16)
        total = jnp.zeros((8, LANES), F32)
        for k in range(0, 8, 2):
            picks = []
            for j in (k, k + 1):
                lane_row = jnp.broadcast_to(lane_at[j:j + 1, :], (LANES, LANES))
                picks.append(jnp.where(lane_id == lane_row, BF16(1), BF16(0)))
            pick = jnp.concatenate(picks, axis=1)
            found = jnp.dot(
                split, jnp.concatenate([pick, pick], axis=0), preferred_element_type=F32
            )
            for j in (0, 1):
                block = found[:, j * LANES:(j + 1) * LANES]
                at = jnp.broadcast_to(rows_at[k + j:k + j + 1, :], (8, LANES))
                bits = [(at & (8 << b)) != 0 for b in range(6)]
                value = choose([block[8 * q:8 * q + 8] for q in range(TABLE // 8)], bits)
                value = jnp.where(sub_id == (at & 7), value, 0.0)
                total = total + value * jnp.broadcast_to(weights[k + j:k + j + 1, :], (8, LANES))
        partial_ref[o] = jnp.sum(total, axis=0, keepdims=True)

    def by_lanes(owners):
        spots = [places(o) for o in owners]
        bits = [[(rows_at & (1 << b)) != 0 for b in range(3)] for rows_at, _, _ in spots]
        found = [jnp.zeros((8, LANES), F32) for _ in owners]
        for q in range(TABLE // 8):
            rows = [table_ref[pl.ds(8 * q + r, 8, stride=0), :] for r in range(8)]
            for i, (rows_at, lane_at, _) in enumerate(spots):
                value = choose([jnp.take_along_axis(row, lane_at, axis=1) for row in rows], bits[i])
                found[i] = jnp.where((rows_at >> 3) == q, value, found[i])
        for o, value, (_, _, weights) in zip(owners, found, spots):
            partial_ref[o] = jnp.sum(value * weights, axis=0, keepdims=True)

    def some(i, _):
        first = i * TURN
        for j in range(TURN - LOOKED_UP):
            by_matmul(first + j)
        for j in range(TURN - LOOKED_UP, TURN, 2):
            by_lanes((first + j, first + j + 1))
        return 0

    lax.fori_loop(0, OWNERS // TURN, some, 0)


def owner_kernel(values_ref, slots_ref, out_ref):
    high_id = iota((32, LANES), 0)
    low_id = iota((LANES, LANES), 0)
    total = jnp.zeros((64, LANES), F32)
    for g in range(0, OWNERS, 8):
        left = []
        right = []
        for j in range(g, g + 8):
            value = values_ref[j]
            slot = slots_ref[pl.ds(j, 1), :]
            coarse = value.astype(BF16).astype(F32)
            fine = value - coarse
            high = high_id == (slot >> 7)
            left.append(
                jnp.concatenate([jnp.where(high, coarse, 0.0), jnp.where(high, fine, 0.0)], axis=0)
            )
            right.append(jnp.where(low_id == (slot & 127), 1.0, 0.0))
        total = total + lax.dot_general(
            jnp.concatenate(left, axis=1).astype(BF16),
            jnp.concatenate(right, axis=1).astype(BF16),
            (((1,), (1,)), ((), ())),
            preferred_element_type=F32,
        )
    out_ref[...] = total[:32] + total[32:]


def shape(*dims):
    return jax.ShapeDtypeStruct(dims, F32)


def shift(array, axis, step, wrap):
    size = lax.axis_size(axis)
    pairs = [(i, (i + step) % size) for i in range(size) if wrap or 0 <= i + step < size]
    return lax.ppermute(array, axis, pairs)


def near(*arrays):
    return [pltpu.with_memory_space_constraint(array, pltpu.MemorySpace.VMEM) for array in arrays]


def local(
    increments, diffusivity, sea_mask, source_cells, source_weights, source_counts, slot_owner
):
    base, first, last = pl.pallas_call(
        pack_kernel,
        in_specs=[VMEM] * 3,
        out_specs=(VMEM,) * 3,
        out_shape=(pltpu.VMEM((ARRAYS, CY, CX), F32),) + (pltpu.VMEM((CY, LANES), F32),) * 2,
        name="pack",
    )(increments.reshape(LAYERS, CY, CX), diffusivity, sea_mask)
    east = shift(first, "gx", -1, True)
    west = shift(last, "gx", 1, True)
    low, high = pl.pallas_call(
        rows_kernel,
        in_specs=[VMEM] * 3,
        out_specs=(VMEM,) * 2,
        out_shape=(pltpu.VMEM((HALO * (ARRAYS + 1), CX), F32),) * 2,
        name="rows",
    )(*near(base, east, west))
    north = shift(low, "gy", -1, False)
    south = shift(high, "gy", 1, False)
    smoothed, partial_value = pl.pallas_call(
        main_kernel,
        in_specs=[VMEM] * 5 + [pl.BlockSpec(memory_space=pl.ANY)] * 3,
        out_specs=(VMEM,) * 2,
        out_shape=(shape(LAYERS, CY, CX), pltpu.VMEM((OWNERS, 1, LANES), F32)),
        scratch_shapes=[
            pltpu.VMEM((ARRAYS, WIDE, ROWS, LANES), F32),
            pltpu.VMEM((LEVELS, 5, BANDS, WIDE, 8, LANES), F32),
            pltpu.VMEM((TABLE, LANES), F32),
            pltpu.VMEM((TABLE, 2 * LANES), BF16),
            pltpu.VMEM((OWNERS, 3, 8, LANES), jnp.int32),
            pltpu.VMEM((OWNERS, 8, LANES), F32),
            pltpu.VMEM((OWNERS, LANES), jnp.int32),
            pltpu.SemaphoreType.DMA((3,)),
        ],
        name="main",
    )(
        *near(base, east, west, north, south),
        source_cells[0],
        source_weights[0],
        source_counts[0],
    )
    received = lax.all_to_all(
        partial_value, ("gx", "gy"), split_axis=0, concat_axis=0, tiled=True
    )
    obs_equiv = pl.pallas_call(
        owner_kernel,
        in_specs=[VMEM] * 2,
        out_specs=VMEM,
        out_shape=shape(OBS_DEV // LANES, LANES),
        name="owner",
    )(*near(received, slot_owner[0]))
    return smoothed.reshape(increments.shape), obs_equiv.reshape(-1)


def solution(mesh):
    return jax.shard_map(
        local,
        mesh=mesh,
        in_specs=(
            P(None, None, "gy", "gx"),
            P(None, "gy", "gx"),
            P("gy", "gx"),
            P(("gx", "gy"), None, None, None, None),
            P(("gx", "gy"), None, None, None),
            P(("gx", "gy"), None, None),
            P(("gx", "gy"), None, None),
        ),
        out_specs=(P(None, None, "gy", "gx"), P(("gx", "gy"))),
        check_vma=False,
    )
```

time: 82 us -> 62 us (0.76)
  Pallas kernels: 41.7 us -> 23.9 us
  local copies, waits for them, and re-layouts: 1.23 us -> 0.01 us
    pallas_call x4, Pallas kernels: 41.7 us -> 23.9 us  [the longest x1 20.6 us: local(): pl.pallas_call(main_kernel, in_specs=[VMEM] * 5 + [pl.BlockSpec(memory_sp...]
    unnamed x8 -> x2, local copies, waits for them, and re-layouts: 1.23 us -> 0.01 us
where the time goes in v2:
time: 62 us; the launch traced here: 61.8 us
  Pallas kernels  23.9 us (39%)
  blocking collectives  17 us (27%)
  starting transfers between devices  13.9 us (22%)
  waiting for transfers between devices  6.35 us (10%)
  between operations  0.68 us (1%)
    pallas_call x1, Pallas kernels, local(): pl.pallas_call(main_kernel, in_specs=[VMEM] * 5 + [pl.BlockSpec(memory_sp...  20.6 us
    all_to_all x1, blocking collectives, local(): lax.all_to_all(partial_value, ('gx', 'gy'), split_axis=0, concat_axis=0,...  17 us
    ppermute x4, starting transfers between devices, shift(): return lax.ppermute(array, axis, pairs)  13.9 us
    ppermute x4, waiting for transfers between devices, shift(): return lax.ppermute(array, axis, pairs)  6.35 us
    pallas_call x1, Pallas kernels, local(): pl.pallas_call(owner_kernel, in_specs=[VMEM] * 2, out_specs=VMEM, out_sha...  2.21 us
  transfers between devices with their start and end apart: 4, of which 4 were waited for; matrix products, arithmetic and copies ran while one was open for 0% of the time, Pallas kernels for 0%

profile of v2, /device:TPU:1, one launch (start us, length us, event | category | flops | bytes accessed | tf_op | source)
XLA Modules:
  0.0 61.8 jit_solution(313466053262964795)
XLA Ops:
  0.6 0.0 copy-start
  0.6 1.1 %pack.1 = (f32[9,24,256]{2,1,0:T(8,128)S(1)}, f32[24,128]{1,0:T(8,128)S(1)}, f32[24,128]{1,0:T(8,128)S(1)}) custom-call(f32[6,24,256]{2,1,0:T(8,128)} %bitcast.10, f32[3,24,256]{2,1,0:T(8,128)} %dif_ref.1, s32[24,256]{1,0:T(8,128)} %mask_ref.1), custom_call_target="tpu_custom_call" | custom-call | tf_op jit(solution)/shard_map/pack/pallas_call | solution.py:300
  1.7 5.6 %collective-permute-start = (f32[24,128]{1,0:T(8,128)S(1)}, f32[24,128]{1,0:T(8,128)S(1)}, u32[]{:S(2)}, u32[]{:S(2)}) collective-permute-start(f32[24,128]{1,0:T(8,128)S(1)} %get-tuple-element.10), channel_id=1, source_target_pairs={{0,112},{16,0},{32,16},{48,32},{64,48},{80,64},{96,80},{112,96},{1... | collective-permute-start | bytes 36872 | tf_op jit(solution)/shard_map/ppermute | solution.py:290
  7.3 0.0 collective-permute-start.1
  7.3 0.8 %collective-permute-done.east_ref = f32[24,128]{1,0:T(8,128)S(1)} collective-permute-done((f32[24,128]{1,0:T(8,128)S(1)}, f32[24,128]{1,0:T(8,128)S(1)}, u32[]{:S(2)}, u32[]{:S(2)}) %collective-permute-start) | collective-permute-done | bytes 12320 | tf_op jit(solution)/shard_map/ppermute | solution.py:290
  8.2 3.8 %collective-permute-done.1.west_ref = f32[24,128]{1,0:T(8,128)S(1)} collective-permute-done((f32[24,128]{1,0:T(8,128)S(1)}, f32[24,128]{1,0:T(8,128)S(1)}, u32[]{:S(2)}, u32[]{:S(2)}) %collective-permute-start.1) | collective-permute-done | bytes 12320 | tf_op jit(solution)/shard_map/ppermute | solution.py:290
  12.0 4.0 %collective-permute-start.2 = (f32[100,256]{1,0:T(8,128)S(1)}, f32[100,256]{1,0:T(8,128)S(1)}, u32[]{:S(2)}, u32[]{:S(2)}) collective-permute-start(f32[100,256]{1,0:T(8,128)S(1)} %get-tuple-element.12), channel_id=1, source_target_pairs={{1,0},{2,1},{3,2},{4,3},{5,4},{6,5},{7,6},{8,7},{9,8},{10,9},{11,1... | collective-permute-start | bytes 307208 | tf_op jit(solution)/shard_map/ppermute | solution.py:290
  16.0 4.3 %collective-permute-start.3 = (f32[100,256]{1,0:T(8,128)S(1)}, f32[100,256]{1,0:T(8,128)S(1)}, u32[]{:S(2)}, u32[]{:S(2)}) collective-permute-start(f32[100,256]{1,0:T(8,128)S(1)} %get-tuple-element.13), channel_id=1, source_target_pairs={{0,1},{1,2},{2,3},{3,4},{4,5},{5,6},{6,7},{7,8},{8,9},{9,10},{10,1... | collective-permute-start | bytes 307208 | tf_op jit(solution)/shard_map/ppermute | solution.py:290
  20.3 0.4 collective-permute-done.2.north_ref
  20.8 1.2 %collective-permute-done.3.south_ref = f32[100,256]{1,0:T(8,128)S(1)} collective-permute-done((f32[100,256]{1,0:T(8,128)S(1)}, f32[100,256]{1,0:T(8,128)S(1)}, u32[]{:S(2)}, u32[]{:S(2)}) %collective-permute-start.3) | collective-permute-done | bytes 102432 | tf_op jit(solution)/shard_map/ppermute | solution.py:290
  22.0 20.6 %main.1 = (f32[6,24,256]{2,1,0:T(8,128)}, f32[128,1,128]{2,1,0:T(1,128)S(1)}) custom-call(f32[9,24,256]{2,1,0:T(8,128)S(1)} %get-tuple-element.9.base_ref, f32[24,128]{1,0:T(8,128)S(1)} %collective-permute-done.east_ref, f32[24,128]{1,0:T(8,128)S(1)} %collective-permute-done.1.west_ref, f32[100,256]{1,0:T(8,128)S(1)} %collective-permute-done.2.north_ref, ...), custom_call_target="tpu_custom_call" | custom-call | tf_op jit(solution)/shard_map/main/pallas_call | solution.py:318
  42.6 17.0 %all_to_all.5.values_ref = f32[128,1,128]{2,1,0:T(1,128)S(1)} all-to-all(f32[128,1,128]{2,1,0:T(1,128)S(1)} %get-tuple-element.15), channel_id=1, replica_groups=mesh['gx'=8,'gy'=16] {'gx','gy'}, dimensions={0} | all-to-all | bytes 131072 | tf_op jit(solution)/shard_map/all_to_all | solution.py:340
  59.6 0.0 copy-done
  59.6 2.2 %owner.1 = f32[32,128]{1,0:T(8,128)} custom-call(f32[128,1,128]{2,1,0:T(1,128)S(1)} %all_to_all.5.values_ref, s32[128,128]{1,0:T(8,128)S(1)} %bitcast.7), custom_call_target="tpu_custom_call" | custom-call | tf_op jit(solution)/shard_map/owner/pallas_call | solution.py:343
  (1 shorter events, 0.0 us)
Async XLA Ops:
  0.6 59.0 %copy-start = (s32[1,128,128]{2,1,0:T(8,128)S(1)}, s32[1,128,128]{2,1,0:T(8,128)}, u32[]{:S(2)}) copy-start(s32[1,128,128]{2,1,0:T(8,128)} %param.13) | copy-start | bytes 196612
  1.7 6.4 %collective-permute-start = (f32[24,128]{1,0:T(8,128)S(1)}, f32[24,128]{1,0:T(8,128)S(1)}, u32[]{:S(2)}, u32[]{:S(2)}) collective-permute-start(f32[24,128]{1,0:T(8,128)S(1)} %get-tuple-element.10), channel_id=1, source_target_pairs={{0,112},{16,0},{32,16},{48,32},{64,48},{80,64},{96,80},{112,96},{1... | collective-permute-start | bytes 36872 | tf_op jit(solution)/shard_map/ppermute | solution.py:290
  7.3 4.7 %collective-permute-start.1 = (f32[24,128]{1,0:T(8,128)S(1)}, f32[24,128]{1,0:T(8,128)S(1)}, u32[]{:S(2)}, u32[]{:S(2)}) collective-permute-start(f32[24,128]{1,0:T(8,128)S(1)} %get-tuple-element.11), channel_id=1, source_target_pairs={{0,16},{16,32},{32,48},{48,64},{64,80},{80,96},{96,112},{112,0},{1... | collective-permute-start | bytes 36872 | tf_op jit(solution)/shard_map/ppermute | solution.py:290
  12.0 8.7 %collective-permute-start.2 = (f32[100,256]{1,0:T(8,128)S(1)}, f32[100,256]{1,0:T(8,128)S(1)}, u32[]{:S(2)}, u32[]{:S(2)}) collective-permute-start(f32[100,256]{1,0:T(8,128)S(1)} %get-tuple-element.12), channel_id=1, source_target_pairs={{1,0},{2,1},{3,2},{4,3},{5,4},{6,5},{7,6},{8,7},{9,8},{10,9},{11,1... | collective-permute-start | bytes 307208 | tf_op jit(solution)/shard_map/ppermute | solution.py:290
  16.0 6.0 %collective-permute-start.3 = (f32[100,256]{1,0:T(8,128)S(1)}, f32[100,256]{1,0:T(8,128)S(1)}, u32[]{:S(2)}, u32[]{:S(2)}) collective-permute-start(f32[100,256]{1,0:T(8,128)S(1)} %get-tuple-element.13), channel_id=1, source_target_pairs={{0,1},{1,2},{2,3},{3,4},{4,5},{5,6},{6,7},{7,8},{8,9},{9,10},{10,1... | collective-permute-start | bytes 307208 | tf_op jit(solution)/shard_map/ppermute | solution.py:290

commit v3 on v2

--- a/solution.py
+++ b/solution.py
@@ -25,6 +25,8 @@
 BANDS = 6
 UNROLL = 5
 OWNERS = 128
+STAGES = 10
+STRIP = (HALO * (ARRAYS + 1), CX)
 VMEM = pl.BlockSpec(memory_space=pltpu.VMEM)
 
 
@@ -52,14 +54,61 @@
     last_ref[...] = last
 
 
-def rows_kernel(base_ref, east_ref, west_ref, low_ref, high_ref):
-    for a in range(ARRAYS + 1):
-        for ref, start in ((low_ref, 0), (high_ref, CY - HALO)):
-            if a < ARRAYS:
-                ref[pl.ds(HALO * a, HALO), :] = base_ref[a, pl.ds(start, HALO), :]
+def rows_kernel(base_ref, east_ref, west_ref, one_ref, two_ref):
+    even = lax.axis_index("gy") % 2 == 0
+
+    def fill(ref, start):
+        for a in range(ARRAYS):
+            ref[pl.ds(HALO * a, HALO), :] = base_ref[a, pl.ds(start, HALO), :]
+        ref[pl.ds(HALO * ARRAYS, HALO), pl.ds(0, LANES)] = east_ref[pl.ds(start, HALO), :]
+        ref[pl.ds(HALO * ARRAYS, HALO), pl.ds(LANES, LANES)] = west_ref[pl.ds(start, HALO), :]
+
+    @pl.when(even)
+    def _():
+        fill(one_ref, CY - HALO)
+        fill(two_ref, 0)
+
+    @pl.when(jnp.logical_not(even))
+    def _():
+        fill(one_ref, 0)
+        fill(two_ref, CY - HALO)
+
+
+def plan_kernel(cells_ref, counts_ref, spots_ref, moves_ref, first_ref, second_ref, shift_ref):
+    before = (iota((OWNERS, OWNERS), 1) < iota((OWNERS, OWNERS), 0)).astype(F32).astype(BF16)
+    held = counts_ref[...].astype(F32).astype(BF16)
+    start = jnp.dot(before, held, preferred_element_type=F32).astype(jnp.int32)
+    shift_ref[...] = 8 * iota((OWNERS, LANES), 0) - start
+    sub_id = iota((8, LANES), 0)
+    nothing = jnp.zeros((8, LANES), jnp.int32)
+    for o in range(OWNERS):
+        col = cells_ref[o, 2]
+        row = (col >> 7) * (LAYERS * CY) + cells_ref[o, 0] * CY + cells_ref[o, 1]
+        spot = (shift_ref[pl.ds(o, 8, stride=0), :] << 16) + (row << 7) + (col & (LANES - 1))
+        first_ref[o] = jnp.where(sub_id < counts_ref[pl.ds(o, 8, stride=0), :], spot, 0)
+        moves_ref[o] = nothing
+    old_ref, new_ref = first_ref, second_ref
+    for bit in range(STAGES):
+        jump = 1 << bit
+        mark = 1 << (16 + bit)
+        if bit == STAGES - 1:
+            new_ref = spots_ref
+        turned = None
+        for o in range(OWNERS):
+            here = old_ref[o]
+            if bit >= 3:
+                source = o + (jump >> 3)
+                there = old_ref[source] if source < OWNERS else nothing
             else:
-                ref[pl.ds(HALO * a, HALO), pl.ds(0, LANES)] = east_ref[pl.ds(start, HALO), :]
-                ref[pl.ds(HALO * a, HALO), pl.ds(LANES, LANES)] = west_ref[pl.ds(start, HALO), :]
+                if turned is None:
+                    turned = pltpu.roll(here, 8 - jump, 0)
+                after = pltpu.roll(old_ref[o + 1], 8 - jump, 0) if o + 1 < OWNERS else nothing
+                there = jnp.where(sub_id < 8 - jump, turned, after)
+                turned = after
+            goes = here & mark
+            moves_ref[o] = moves_ref[o] | (goes >> 16)
+            new_ref[o] = jnp.where((there & mark) != 0, there, jnp.where(goes != 0, 0, here))
+        old_ref, new_ref = new_ref, old_ref
 
 
 def smooth(
@@ -176,18 +225,23 @@
 
 
 def main_kernel(
-    base_ref, east_ref, west_ref, north_ref, south_ref, cells_far, weights_far, counts_far,
-    smooth_ref, partial_ref, wide_ref, coeff_ref, table_ref, split_ref, cells_ref, weights_ref,
-    counts_ref, arrived,
+    base_ref, east_ref, west_ref, one_ref, two_ref, spots_ref, moves_ref, weights_far, counts_far,
+    smooth_ref, partial_ref, wide_ref, coeff_ref, table_ref, split_ref, north_ref, south_ref,
+    first_ref, second_ref, weights_ref, counts_ref, arrived,
 ):
     fetches = [
         pltpu.make_async_copy(far, ref, arrived.at[i])
-        for i, (far, ref) in enumerate(
-            ((cells_far, cells_ref), (weights_far, weights_ref), (counts_far, counts_ref))
-        )
+        for i, (far, ref) in enumerate(((weights_far, weights_ref), (counts_far, counts_ref)))
     ]
     for fetch in fetches:
         fetch.start()
+    place = lax.axis_index("gy")
+    even = place % 2 == 0
+    edge = (place == 0) | (place == lax.axis_size("gy") - 1)
+    one = one_ref[...]
+    two = jnp.where(edge, 0.0, two_ref[...])
+    north_ref[...] = jnp.where(even, one, two)
+    south_ref[...] = jnp.where(even, two, one)
     smooth(
         base_ref, east_ref, west_ref, north_ref, south_ref, smooth_ref, wide_ref, coeff_ref,
         table_ref,
@@ -199,20 +253,21 @@
 
     for fetch in fetches:
         fetch.wait()
+    counts = counts_ref[...]
+    rows_used = jnp.max(jnp.sum(counts.astype(F32), axis=0, keepdims=True)).astype(jnp.int32)
+    groups = (rows_used + (8 * TURN - 1)) // (8 * TURN)
     split = split_ref[...]
     lane_id = iota((LANES, LANES), 0).astype(BF16)
     sub_id = iota((8, LANES), 0)
 
     def places(o):
-        col = cells_ref[o, 2]
-        rows_at = (col >> 7) * (LAYERS * CY) + cells_ref[o, 0] * CY + cells_ref[o, 1]
-        weights = jnp.where(sub_id < counts_ref[pl.ds(o, 1), :], weights_ref[o], 0.0)
-        return rows_at, col & (LANES - 1), weights
+        spot = spots_ref[o] & 0xFFFF
+        return spot >> 7, spot & (LANES - 1)
 
     def by_matmul(o):
-        rows_at, lane_at, weights = places(o)
+        rows_at, lane_at = places(o)
         lane_at = lane_at.astype(F32).astype(BF16)
-        total = jnp.zeros((8, LANES), F32)
+        result = jnp.zeros((8, LANES), F32)
         for k in range(0, 8, 2):
             picks = []
             for j in (k, k + 1):
@@ -227,21 +282,21 @@
                 at = jnp.broadcast_to(rows_at[k + j:k + j + 1, :], (8, LANES))
                 bits = [(at & (8 << b)) != 0 for b in range(6)]
                 value = choose([block[8 * q:8 * q + 8] for q in range(TABLE // 8)], bits)
-                value = jnp.where(sub_id == (at & 7), value, 0.0)
-                total = total + value * jnp.broadcast_to(weights[k + j:k + j + 1, :], (8, LANES))
-        partial_ref[o] = jnp.sum(total, axis=0, keepdims=True)
+                value = jnp.take_along_axis(value, at & 7, axis=0)
+                result = jnp.where(sub_id == k + j, value, result)
+        first_ref[o] = result
 
     def by_lanes(owners):
         spots = [places(o) for o in owners]
-        bits = [[(rows_at & (1 << b)) != 0 for b in range(3)] for rows_at, _, _ in spots]
+        bits = [[(rows_at & (1 << b)) != 0 for b in range(3)] for rows_at, _ in spots]
         found = [jnp.zeros((8, LANES), F32) for _ in owners]
         for q in range(TABLE // 8):
             rows = [table_ref[pl.ds(8 * q + r, 8, stride=0), :] for r in range(8)]
-            for i, (rows_at, lane_at, _) in enumerate(spots):
+            for i, (rows_at, lane_at) in enumerate(spots):
                 value = choose([jnp.take_along_axis(row, lane_at, axis=1) for row in rows], bits[i])
                 found[i] = jnp.where((rows_at >> 3) == q, value, found[i])
-        for o, value, (_, _, weights) in zip(owners, found, spots):
-            partial_ref[o] = jnp.sum(value * weights, axis=0, keepdims=True)
+        for o, value in zip(owners, found):
+            first_ref[o] = value
 
     def some(i, _):
         first = i * TURN
@@ -251,7 +306,29 @@
             by_lanes((first + j, first + j + 1))
         return 0
 
-    lax.fori_loop(0, OWNERS // TURN, some, 0)
+    lax.fori_loop(0, groups, some, 0)
+
+    old_ref, new_ref = first_ref, second_ref
+    for bit in reversed(range(STAGES)):
+        jump = 1 << bit
+        turned = None
+        for o in range(OWNERS):
+            here = old_ref[o]
+            if bit >= 3:
+                source = o - (jump >> 3)
+                there = old_ref[source] if source >= 0 else here
+            else:
+                now = pltpu.roll(here, jump, 0)
+                there = now if turned is None else jnp.where(sub_id < jump, turned, now)
+                turned = now
+            new = jnp.where((moves_ref[o] & jump) != 0, there, here)
+            if bit:
+                new_ref[o] = new
+            else:
+                valid = sub_id < counts_ref[pl.ds(o, 8, stride=0), :]
+                weighted = jnp.where(valid, weights_ref[o] * new, 0.0)
+                partial_ref[o] = jnp.sum(weighted, axis=0, keepdims=True)
+        old_ref, new_ref = new_ref, old_ref
 
 
 def owner_kernel(values_ref, slots_ref, out_ref):
@@ -284,10 +361,15 @@
     return jax.ShapeDtypeStruct(dims, F32)
 
 
-def shift(array, axis, step, wrap):
+def shift(array, axis, step):
     size = lax.axis_size(axis)
-    pairs = [(i, (i + step) % size) for i in range(size) if wrap or 0 <= i + step < size]
-    return lax.ppermute(array, axis, pairs)
+    return lax.ppermute(array, axis, [(i, (i + step) % size) for i in range(size)])
+
+
+def pairs(array, axis, odd):
+    size = lax.axis_size(axis)
+    swaps = [(i, (((i + odd) % size) ^ 1) - odd) for i in range(size)]
+    return lax.ppermute(array, axis, [(i, j % size) for i, j in swaps])
 
 
 def near(*arrays):
@@ -304,20 +386,29 @@
         out_shape=(pltpu.VMEM((ARRAYS, CY, CX), F32),) + (pltpu.VMEM((CY, LANES), F32),) * 2,
         name="pack",
     )(increments.reshape(LAYERS, CY, CX), diffusivity, sea_mask)
-    east = shift(first, "gx", -1, True)
-    west = shift(last, "gx", 1, True)
-    low, high = pl.pallas_call(
+    east = shift(first, "gx", -1)
+    west = shift(last, "gx", 1)
+    one, two = pl.pallas_call(
         rows_kernel,
         in_specs=[VMEM] * 3,
         out_specs=(VMEM,) * 2,
-        out_shape=(pltpu.VMEM((HALO * (ARRAYS + 1), CX), F32),) * 2,
+        out_shape=(pltpu.VMEM(STRIP, F32),) * 2,
         name="rows",
     )(*near(base, east, west))
-    north = shift(low, "gy", -1, False)
-    south = shift(high, "gy", 1, False)
+    one = pairs(one, "gy", 0)
+    two = pairs(two, "gy", 1)
+    whole = pltpu.VMEM((OWNERS, 8, LANES), jnp.int32)
+    spots, moves = pl.pallas_call(
+        plan_kernel,
+        in_specs=[VMEM] * 2,
+        out_specs=(VMEM,) * 2,
+        out_shape=(whole, whole),
+        scratch_shapes=[whole, whole, pltpu.VMEM((OWNERS, LANES), jnp.int32)],
+        name="plan",
+    )(source_cells[0], source_counts[0])
     smoothed, partial_value = pl.pallas_call(
         main_kernel,
-        in_specs=[VMEM] * 5 + [pl.BlockSpec(memory_space=pl.ANY)] * 3,
+        in_specs=[VMEM] * 7 + [pl.BlockSpec(memory_space=pl.ANY)] * 2,
         out_specs=(VMEM,) * 2,
         out_shape=(shape(LAYERS, CY, CX), pltpu.VMEM((OWNERS, 1, LANES), F32)),
         scratch_shapes=[
@@ -325,18 +416,16 @@
             pltpu.VMEM((LEVELS, 5, BANDS, WIDE, 8, LANES), F32),
             pltpu.VMEM((TABLE, LANES), F32),
             pltpu.VMEM((TABLE, 2 * LANES), BF16),
-            pltpu.VMEM((OWNERS, 3, 8, LANES), jnp.int32),
+            pltpu.VMEM(STRIP, F32),
+            pltpu.VMEM(STRIP, F32),
+            pltpu.VMEM((OWNERS, 8, LANES), F32),
+            pltpu.VMEM((OWNERS, 8, LANES), F32),
             pltpu.VMEM((OWNERS, 8, LANES), F32),
             pltpu.VMEM((OWNERS, LANES), jnp.int32),
-            pltpu.SemaphoreType.DMA((3,)),
+            pltpu.SemaphoreType.DMA((2,)),
         ],
         name="main",
-    )(
-        *near(base, east, west, north, south),
-        source_cells[0],
-        source_weights[0],
-        source_counts[0],
-    )
+    )(*near(base, east, west, one, two, spots, moves), source_weights[0], source_counts[0])
     received = lax.all_to_all(
         partial_value, ("gx", "gy"), split_axis=0, concat_axis=0, tiled=True
     )

time: 62 us -> 54.7 us (0.88)
  starting transfers between devices: 13.9 us -> 10.2 us
  Pallas kernels: 23.9 us -> 21.4 us
    ppermute x4, starting transfers between devices: 13.9 us -> 10.2 us  [the longest x2 5.59 us: shift(): lax.ppermute(array, axis, [(i, (i + step) % size) for i in range(size)])]
    pallas_call x1 -> x2, Pallas kernels: 20.6 us -> 18.1 us  [the longest x1 15 us: local(): pl.pallas_call(main_kernel, in_specs=[VMEM] * 7 + [pl.BlockSpec(memory_sp...]
    all_to_all x1, blocking collectives: 17 us -> 16.4 us  [local(): lax.all_to_all(partial_value, ('gx', 'gy'), split_axis=0, concat_axis=0,...]
  transfers between devices with their start and end apart: 4 -> 4, of which waited for: 4 -> 3; matrix products, arithmetic and copies ran while one was open for 0% -> 0% of each run, Pallas kernels for 0% -> 6%
where the time goes in v3:
time: 54.7 us; the launch traced here: 54.6 us
  Pallas kernels  21.4 us (39%)
  blocking collectives  16.4 us (30%)
  starting transfers between devices  10.2 us (19%)
  waiting for transfers between devices  5.92 us (11%)
  between operations  0.67 us (1%)
    all_to_all x1, blocking collectives, local(): lax.all_to_all(partial_value, ('gx', 'gy'), split_axis=0, concat_axis=0,...  16.4 us
    pallas_call x1, Pallas kernels, local(): pl.pallas_call(main_kernel, in_specs=[VMEM] * 7 + [pl.BlockSpec(memory_sp...  15 us
    ppermute x2, starting transfers between devices, shift(): lax.ppermute(array, axis, [(i, (i + step) % size) for i in range(size)])  5.59 us
    ppermute x2, waiting for transfers between devices, shift(): lax.ppermute(array, axis, [(i, (i + step) % size) for i in range(size)])  4.65 us
    ppermute x2, starting transfers between devices, pairs(): return lax.ppermute(array, axis, [(i, j % size) for i, j in swaps])  4.62 us
    pallas_call x1, Pallas kernels, local(): pl.pallas_call(plan_kernel, in_specs=[VMEM] * 2, out_specs=(VMEM,) * 2, o...  3.02 us
    pallas_call x1, Pallas kernels, local(): pl.pallas_call(owner_kernel, in_specs=[VMEM] * 2, out_specs=VMEM, out_sha...  2.21 us
    ppermute x2, waiting for transfers between devices, pairs(): return lax.ppermute(array, axis, [(i, j % size) for i, j in swaps])  1.27 us
  transfers between devices with their start and end apart: 4, of which 3 were waited for; matrix products, arithmetic and copies ran while one was open for 0% of the time, Pallas kernels for 6%

profile of v3, /device:TPU:1, one launch (start us, length us, event | category | flops | bytes accessed | tf_op | source)
XLA Modules:
  0.0 54.6 jit_solution(16509809218798556595)
XLA Ops:
  0.6 1.1 %pack.1 = (f32[9,24,256]{2,1,0:T(8,128)S(1)}, f32[24,128]{1,0:T(8,128)S(1)}, f32[24,128]{1,0:T(8,128)S(1)}) custom-call(f32[6,24,256]{2,1,0:T(8,128)} %bitcast.12, f32[3,24,256]{2,1,0:T(8,128)} %dif_ref.1, s32[24,256]{1,0:T(8,128)} %mask_ref.1), custom_call_target="tpu_custom_call" | custom-call | tf_op jit(solution)/shard_map/pack/pallas_call | solution.py:382
  1.7 5.6 %collective-permute-start = (f32[24,128]{1,0:T(8,128)S(1)}, f32[24,128]{1,0:T(8,128)S(1)}, u32[]{:S(2)}, u32[]{:S(2)}) collective-permute-start(f32[24,128]{1,0:T(8,128)S(1)} %get-tuple-element.12), channel_id=1, source_target_pairs={{0,112},{16,0},{32,16},{48,32},{64,48},{80,64},{96,80},{112,96},{1... | collective-permute-start | bytes 36872 | tf_op jit(solution)/shard_map/ppermute | solution.py:366
  7.3 0.0 collective-permute-start.1
  7.3 0.8 %collective-permute-done.east_ref = f32[24,128]{1,0:T(8,128)S(1)} collective-permute-done((f32[24,128]{1,0:T(8,128)S(1)}, f32[24,128]{1,0:T(8,128)S(1)}, u32[]{:S(2)}, u32[]{:S(2)}) %collective-permute-start) | collective-permute-done | bytes 12320 | tf_op jit(solution)/shard_map/ppermute | solution.py:366
  8.1 3.8 %collective-permute-done.1.west_ref = f32[24,128]{1,0:T(8,128)S(1)} collective-permute-done((f32[24,128]{1,0:T(8,128)S(1)}, f32[24,128]{1,0:T(8,128)S(1)}, u32[]{:S(2)}, u32[]{:S(2)}) %collective-permute-start.1) | collective-permute-done | bytes 12320 | tf_op jit(solution)/shard_map/ppermute | solution.py:366
  12.0 2.2 %collective-permute-start.2 = (f32[100,256]{1,0:T(8,128)S(1)}, f32[100,256]{1,0:T(8,128)S(1)}, u32[]{:S(2)}, u32[]{:S(2)}) collective-permute-start(f32[100,256]{1,0:T(8,128)S(1)} %get-tuple-element.14), channel_id=1, source_target_pairs={{0,1},{1,0},{2,3},{3,2},{4,5},{5,4},{6,7},{7,6},{8,9},{9,8},{10,11... | collective-permute-start | bytes 307208 | tf_op jit(solution)/shard_map/ppermute | solution.py:372
  14.2 2.4 %collective-permute-start.3 = (f32[100,256]{1,0:T(8,128)S(1)}, f32[100,256]{1,0:T(8,128)S(1)}, u32[]{:S(2)}, u32[]{:S(2)}) collective-permute-start(f32[100,256]{1,0:T(8,128)S(1)} %get-tuple-element.15), channel_id=1, source_target_pairs={{0,15},{1,2},{2,1},{3,4},{4,3},{5,6},{6,5},{7,8},{8,7},{9,10},{10,... | collective-permute-start | bytes 307208 | tf_op jit(solution)/shard_map/ppermute | solution.py:372
  16.6 0.0 copy-start
  16.6 3.0 %plan.1 = (s32[128,8,128]{2,1,0:T(8,128)S(1)}, s32[128,8,128]{2,1,0:T(8,128)S(1)}) custom-call(s32[128,3,8,128]{3,2,1,0:T(8,128)} %bitcast.8, s32[128,128]{1,0:T(8,128)} %bitcast.10), custom_call_target="tpu_custom_call" | custom-call | tf_op jit(solution)/shard_map/plan/pallas_call | solution.py:401
  19.6 0.0 collective-permute-done.2.one_ref
  19.6 1.3 %collective-permute-done.3.two_ref = f32[100,256]{1,0:T(8,128)S(1)} collective-permute-done((f32[100,256]{1,0:T(8,128)S(1)}, f32[100,256]{1,0:T(8,128)S(1)}, u32[]{:S(2)}, u32[]{:S(2)}) %collective-permute-start.3) | collective-permute-done | bytes 102432 | tf_op jit(solution)/shard_map/ppermute | solution.py:372
  20.9 15.0 %main.1 = (f32[6,24,256]{2,1,0:T(8,128)}, f32[128,1,128]{2,1,0:T(1,128)S(1)}) custom-call(f32[9,24,256]{2,1,0:T(8,128)S(1)} %get-tuple-element.11.base_ref, f32[24,128]{1,0:T(8,128)S(1)} %collective-permute-done.east_ref, f32[24,128]{1,0:T(8,128)S(1)} %collective-permute-done.1.west_ref, f32[100,256]{1,0:T(8,128)S(1)} %collective-permute-done.2.one_ref, ...), custom_call_target="tpu_custom_call" | custom-call | tf_op jit(solution)/shard_map/main/pallas_call | solution.py:409
  36.0 16.4 %all_to_all.5.values_ref = f32[128,1,128]{2,1,0:T(1,128)S(1)} all-to-all(f32[128,1,128]{2,1,0:T(1,128)S(1)} %get-tuple-element.19), channel_id=1, replica_groups=mesh['gx'=8,'gy'=16] {'gx','gy'}, dimensions={0} | all-to-all | bytes 131072 | tf_op jit(solution)/shard_map/all_to_all | solution.py:429
  52.3 0.0 copy-done
  52.3 2.2 %owner.1 = f32[32,128]{1,0:T(8,128)} custom-call(f32[128,1,128]{2,1,0:T(1,128)S(1)} %all_to_all.5.values_ref, s32[128,128]{1,0:T(8,128)S(1)} %bitcast.7), custom_call_target="tpu_custom_call" | custom-call | tf_op jit(solution)/shard_map/owner/pallas_call | solution.py:432
  (1 shorter events, 0.0 us)
Async XLA Ops:
  1.7 6.4 %collective-permute-start = (f32[24,128]{1,0:T(8,128)S(1)}, f32[24,128]{1,0:T(8,128)S(1)}, u32[]{:S(2)}, u32[]{:S(2)}) collective-permute-start(f32[24,128]{1,0:T(8,128)S(1)} %get-tuple-element.12), channel_id=1, source_target_pairs={{0,112},{16,0},{32,16},{48,32},{64,48},{80,64},{96,80},{112,96},{1... | collective-permute-start | bytes 36872 | tf_op jit(solution)/shard_map/ppermute | solution.py:366
  7.3 4.7 %collective-permute-start.1 = (f32[24,128]{1,0:T(8,128)S(1)}, f32[24,128]{1,0:T(8,128)S(1)}, u32[]{:S(2)}, u32[]{:S(2)}) collective-permute-start(f32[24,128]{1,0:T(8,128)S(1)} %get-tuple-element.13), channel_id=1, source_target_pairs={{0,16},{16,32},{32,48},{48,64},{64,80},{80,96},{96,112},{112,0},{1... | collective-permute-start | bytes 36872 | tf_op jit(solution)/shard_map/ppermute | solution.py:366
  12.0 7.7 %collective-permute-start.2 = (f32[100,256]{1,0:T(8,128)S(1)}, f32[100,256]{1,0:T(8,128)S(1)}, u32[]{:S(2)}, u32[]{:S(2)}) collective-permute-start(f32[100,256]{1,0:T(8,128)S(1)} %get-tuple-element.14), channel_id=1, source_target_pairs={{0,1},{1,0},{2,3},{3,2},{4,5},{5,4},{6,7},{7,6},{8,9},{9,8},{10,11... | collective-permute-start | bytes 307208 | tf_op jit(solution)/shard_map/ppermute | solution.py:372
  14.2 6.7 %collective-permute-start.3 = (f32[100,256]{1,0:T(8,128)S(1)}, f32[100,256]{1,0:T(8,128)S(1)}, u32[]{:S(2)}, u32[]{:S(2)}) collective-permute-start(f32[100,256]{1,0:T(8,128)S(1)} %get-tuple-element.15), channel_id=1, source_target_pairs={{0,15},{1,2},{2,1},{3,4},{4,3},{5,6},{6,5},{7,8},{8,7},{9,10},{10,... | collective-permute-start | bytes 307208 | tf_op jit(solution)/shard_map/ppermute | solution.py:372
  16.6 35.7 %copy-start = (s32[1,128,128]{2,1,0:T(8,128)S(1)}, s32[1,128,128]{2,1,0:T(8,128)}, u32[]{:S(2)}) copy-start(s32[1,128,128]{2,1,0:T(8,128)} %param.13) | copy-start | bytes 196612

commit v4 on v3

--- a/solution.py
+++ b/solution.py
@@ -21,7 +21,7 @@
 WIDE = 3
 TABLE = LAYERS * CY * 2
 TURN = 16
-LOOKED_UP = 4
+LOOKED_UP = 5
 BANDS = 6
 UNROLL = 5
 OWNERS = 128
@@ -226,8 +226,8 @@
 
 def main_kernel(
     base_ref, east_ref, west_ref, one_ref, two_ref, spots_ref, moves_ref, weights_far, counts_far,
-    smooth_ref, partial_ref, wide_ref, coeff_ref, table_ref, split_ref, north_ref, south_ref,
-    first_ref, second_ref, weights_ref, counts_ref, arrived,
+    smooth_far, partial_ref, wide_ref, coeff_ref, table_ref, split_ref, north_ref, south_ref,
+    first_ref, second_ref, weights_ref, counts_ref, smooth_ref, arrived,
 ):
     fetches = [
         pltpu.make_async_copy(far, ref, arrived.at[i])
@@ -246,6 +246,8 @@
         base_ref, east_ref, west_ref, north_ref, south_ref, smooth_ref, wide_ref, coeff_ref,
         table_ref,
     )
+    leave = pltpu.make_async_copy(smooth_ref, smooth_far, arrived.at[2])
+    leave.start()
     values = table_ref[...]
     coarse = values.astype(BF16)
     split_ref[:, pl.ds(0, LANES)] = coarse
@@ -286,24 +288,22 @@
                 result = jnp.where(sub_id == k + j, value, result)
         first_ref[o] = result
 
-    def by_lanes(owners):
-        spots = [places(o) for o in owners]
-        bits = [[(rows_at & (1 << b)) != 0 for b in range(3)] for rows_at, _ in spots]
-        found = [jnp.zeros((8, LANES), F32) for _ in owners]
+    def by_lanes(o):
+        rows_at, lane_at = places(o)
+        bits = [(rows_at & (1 << b)) != 0 for b in range(3)]
+        found = jnp.zeros((8, LANES), F32)
         for q in range(TABLE // 8):
             rows = [table_ref[pl.ds(8 * q + r, 8, stride=0), :] for r in range(8)]
-            for i, (rows_at, lane_at) in enumerate(spots):
-                value = choose([jnp.take_along_axis(row, lane_at, axis=1) for row in rows], bits[i])
-                found[i] = jnp.where((rows_at >> 3) == q, value, found[i])
-        for o, value in zip(owners, found):
-            first_ref[o] = value
+            value = choose([jnp.take_along_axis(row, lane_at, axis=1) for row in rows], bits)
+            found = jnp.where((rows_at >> 3) == q, value, found)
+        first_ref[o] = found
 
     def some(i, _):
         first = i * TURN
         for j in range(TURN - LOOKED_UP):
             by_matmul(first + j)
-        for j in range(TURN - LOOKED_UP, TURN, 2):
-            by_lanes((first + j, first + j + 1))
+        for j in range(TURN - LOOKED_UP, TURN):
+            by_lanes(first + j)
         return 0
 
     lax.fori_loop(0, groups, some, 0)
@@ -329,31 +329,39 @@
                 weighted = jnp.where(valid, weights_ref[o] * new, 0.0)
                 partial_ref[o] = jnp.sum(weighted, axis=0, keepdims=True)
         old_ref, new_ref = new_ref, old_ref
+    leave.wait()
 
 
 def owner_kernel(values_ref, slots_ref, out_ref):
-    high_id = iota((32, LANES), 0)
-    low_id = iota((LANES, LANES), 0)
-    total = jnp.zeros((64, LANES), F32)
+    high_id = iota((32, LANES), 0).astype(BF16)
+    low_id = iota((LANES, LANES), 0).astype(BF16)
+    slots = slots_ref[...]
+    highs = (slots >> 7).astype(F32).astype(BF16)
+    lows = (slots & (LANES - 1)).astype(F32).astype(BF16)
+    none = jnp.zeros((32, LANES), BF16)
+    total = jnp.zeros((LANES, 64), F32)
     for g in range(0, OWNERS, 8):
         left = []
         right = []
         for j in range(g, g + 8):
             value = values_ref[j]
-            slot = slots_ref[pl.ds(j, 1), :]
-            coarse = value.astype(BF16).astype(F32)
-            fine = value - coarse
-            high = high_id == (slot >> 7)
-            left.append(
-                jnp.concatenate([jnp.where(high, coarse, 0.0), jnp.where(high, fine, 0.0)], axis=0)
-            )
-            right.append(jnp.where(low_id == (slot & 127), 1.0, 0.0))
+            coarse = value.astype(BF16)
+            fine = (value - coarse.astype(F32)).astype(BF16)
+            high = high_id == jnp.broadcast_to(highs[j:j + 1, :], (32, LANES))
+            low = low_id == jnp.broadcast_to(lows[j:j + 1, :], (LANES, LANES))
+            parts = [
+                jnp.where(high, jnp.broadcast_to(part, (32, LANES)), none)
+                for part in (coarse, fine)
+            ]
+            right.append(jnp.concatenate(parts, axis=0))
+            left.append(jnp.where(low, BF16(1), BF16(0)))
         total = total + lax.dot_general(
-            jnp.concatenate(left, axis=1).astype(BF16),
-            jnp.concatenate(right, axis=1).astype(BF16),
+            jnp.concatenate(left, axis=1),
+            jnp.concatenate(right, axis=1),
             (((1,), (1,)), ((), ())),
             preferred_element_type=F32,
         )
+    total = total.T
     out_ref[...] = total[:32] + total[32:]
 
 
@@ -409,7 +417,7 @@
     smoothed, partial_value = pl.pallas_call(
         main_kernel,
         in_specs=[VMEM] * 7 + [pl.BlockSpec(memory_space=pl.ANY)] * 2,
-        out_specs=(VMEM,) * 2,
+        out_specs=(pl.BlockSpec(memory_space=pl.ANY), VMEM),
         out_shape=(shape(LAYERS, CY, CX), pltpu.VMEM((OWNERS, 1, LANES), F32)),
         scratch_shapes=[
             pltpu.VMEM((ARRAYS, WIDE, ROWS, LANES), F32),
@@ -422,7 +430,8 @@
             pltpu.VMEM((OWNERS, 8, LANES), F32),
             pltpu.VMEM((OWNERS, 8, LANES), F32),
             pltpu.VMEM((OWNERS, LANES), jnp.int32),
-            pltpu.SemaphoreType.DMA((2,)),
+            pltpu.VMEM((LAYERS, CY, CX), F32),
+            pltpu.SemaphoreType.DMA((3,)),
         ],
         name="main",
     )(*near(base, east, west, one, two, spots, moves), source_weights[0], source_counts[0])

time: 54.7 us -> 53.6 us (0.980)
  Pallas kernels: 21.4 us -> 20.3 us
    pallas_call x1, Pallas kernels: 15 us -> 14.2 us  [local(): pl.pallas_call(main_kernel, in_specs=[VMEM] * 7 + [pl.BlockSpec(memory_sp...]
where the time goes in v4:
time: 53.6 us; the launch traced here: 53.4 us
  Pallas kernels  20.3 us (38%)
  blocking collectives  16.4 us (31%)
  starting transfers between devices  10.2 us (19%)
  waiting for transfers between devices  5.92 us (11%)
  between operations  0.67 us (1%)
    all_to_all x1, blocking collectives, local(): lax.all_to_all(partial_value, ('gx', 'gy'), split_axis=0, concat_axis=0,...  16.4 us
    pallas_call x1, Pallas kernels, local(): pl.pallas_call(main_kernel, in_specs=[VMEM] * 7 + [pl.BlockSpec(memory_sp...  14.2 us
    ppermute x2, starting transfers between devices, shift(): lax.ppermute(array, axis, [(i, (i + step) % size) for i in range(size)])  5.59 us
    ppermute x2, waiting for transfers between devices, shift(): lax.ppermute(array, axis, [(i, (i + step) % size) for i in range(size)])  4.65 us
    ppermute x2, starting transfers between devices, pairs(): return lax.ppermute(array, axis, [(i, j % size) for i, j in swaps])  4.62 us
    pallas_call x1, Pallas kernels, local(): pl.pallas_call(plan_kernel, in_specs=[VMEM] * 2, out_specs=(VMEM,) * 2, o...  3.02 us
    pallas_call x1, Pallas kernels, local(): pl.pallas_call(owner_kernel, in_specs=[VMEM] * 2, out_specs=VMEM, out_sha...  1.9 us
    ppermute x2, waiting for transfers between devices, pairs(): return lax.ppermute(array, axis, [(i, j % size) for i, j in swaps])  1.27 us
  transfers between devices with their start and end apart: 4, of which 3 were waited for; matrix products, arithmetic and copies ran while one was open for 0% of the time, Pallas kernels for 6%

profile of v4, /device:TPU:1, one launch (start us, length us, event | category | flops | bytes accessed | tf_op | source)
XLA Modules:
  0.0 53.4 jit_solution(2928462729148694767)
XLA Ops:
  0.6 1.1 %pack.1 = (f32[9,24,256]{2,1,0:T(8,128)S(1)}, f32[24,128]{1,0:T(8,128)S(1)}, f32[24,128]{1,0:T(8,128)S(1)}) custom-call(f32[6,24,256]{2,1,0:T(8,128)} %bitcast.12, f32[3,24,256]{2,1,0:T(8,128)} %dif_ref.1, s32[24,256]{1,0:T(8,128)} %mask_ref.1), custom_call_target="tpu_custom_call" | custom-call | tf_op jit(solution)/shard_map/pack/pallas_call | solution.py:390
  1.7 5.6 %collective-permute-start = (f32[24,128]{1,0:T(8,128)S(1)}, f32[24,128]{1,0:T(8,128)S(1)}, u32[]{:S(2)}, u32[]{:S(2)}) collective-permute-start(f32[24,128]{1,0:T(8,128)S(1)} %get-tuple-element.12), channel_id=1, source_target_pairs={{0,112},{16,0},{32,16},{48,32},{64,48},{80,64},{96,80},{112,96},{1... | collective-permute-start | bytes 36872 | tf_op jit(solution)/shard_map/ppermute | solution.py:374
  7.3 0.0 collective-permute-start.1
  7.3 0.8 %collective-permute-done.east_ref = f32[24,128]{1,0:T(8,128)S(1)} collective-permute-done((f32[24,128]{1,0:T(8,128)S(1)}, f32[24,128]{1,0:T(8,128)S(1)}, u32[]{:S(2)}, u32[]{:S(2)}) %collective-permute-start) | collective-permute-done | bytes 12320 | tf_op jit(solution)/shard_map/ppermute | solution.py:374
  8.1 3.8 %collective-permute-done.1.west_ref = f32[24,128]{1,0:T(8,128)S(1)} collective-permute-done((f32[24,128]{1,0:T(8,128)S(1)}, f32[24,128]{1,0:T(8,128)S(1)}, u32[]{:S(2)}, u32[]{:S(2)}) %collective-permute-start.1) | collective-permute-done | bytes 12320 | tf_op jit(solution)/shard_map/ppermute | solution.py:374
  12.0 2.2 %collective-permute-start.2 = (f32[100,256]{1,0:T(8,128)S(1)}, f32[100,256]{1,0:T(8,128)S(1)}, u32[]{:S(2)}, u32[]{:S(2)}) collective-permute-start(f32[100,256]{1,0:T(8,128)S(1)} %get-tuple-element.14), channel_id=1, source_target_pairs={{0,1},{1,0},{2,3},{3,2},{4,5},{5,4},{6,7},{7,6},{8,9},{9,8},{10,11... | collective-permute-start | bytes 307208 | tf_op jit(solution)/shard_map/ppermute | solution.py:380
  14.2 2.4 %collective-permute-start.3 = (f32[100,256]{1,0:T(8,128)S(1)}, f32[100,256]{1,0:T(8,128)S(1)}, u32[]{:S(2)}, u32[]{:S(2)}) collective-permute-start(f32[100,256]{1,0:T(8,128)S(1)} %get-tuple-element.15), channel_id=1, source_target_pairs={{0,15},{1,2},{2,1},{3,4},{4,3},{5,6},{6,5},{7,8},{8,7},{9,10},{10,... | collective-permute-start | bytes 307208 | tf_op jit(solution)/shard_map/ppermute | solution.py:380
  16.6 0.0 copy-start
  16.6 3.0 %plan.1 = (s32[128,8,128]{2,1,0:T(8,128)S(1)}, s32[128,8,128]{2,1,0:T(8,128)S(1)}) custom-call(s32[128,3,8,128]{3,2,1,0:T(8,128)} %bitcast.8, s32[128,128]{1,0:T(8,128)} %bitcast.10), custom_call_target="tpu_custom_call" | custom-call | tf_op jit(solution)/shard_map/plan/pallas_call | solution.py:409
  19.6 0.0 collective-permute-done.2.one_ref
  19.6 1.3 %collective-permute-done.3.two_ref = f32[100,256]{1,0:T(8,128)S(1)} collective-permute-done((f32[100,256]{1,0:T(8,128)S(1)}, f32[100,256]{1,0:T(8,128)S(1)}, u32[]{:S(2)}, u32[]{:S(2)}) %collective-permute-start.3) | collective-permute-done | bytes 102432 | tf_op jit(solution)/shard_map/ppermute | solution.py:380
  20.9 14.2 %main.1 = (f32[6,24,256]{2,1,0:T(8,128)}, f32[128,1,128]{2,1,0:T(1,128)S(1)}) custom-call(f32[9,24,256]{2,1,0:T(8,128)S(1)} %get-tuple-element.11.base_ref, f32[24,128]{1,0:T(8,128)S(1)} %collective-permute-done.east_ref, f32[24,128]{1,0:T(8,128)S(1)} %collective-permute-done.1.west_ref, f32[100,256]{1,0:T(8,128)S(1)} %collective-permute-done.2.one_ref, ...), custom_call_target="tpu_custom_call" | custom-call | tf_op jit(solution)/shard_map/main/pallas_call | solution.py:417
  35.1 16.4 %all_to_all.5.values_ref = f32[128,1,128]{2,1,0:T(1,128)S(1)} all-to-all(f32[128,1,128]{2,1,0:T(1,128)S(1)} %get-tuple-element.19), channel_id=1, replica_groups=mesh['gx'=8,'gy'=16] {'gx','gy'}, dimensions={0} | all-to-all | bytes 131072 | tf_op jit(solution)/shard_map/all_to_all | solution.py:438
  51.5 0.0 copy-done
  51.5 1.9 %owner.1 = f32[32,128]{1,0:T(8,128)} custom-call(f32[128,1,128]{2,1,0:T(1,128)S(1)} %all_to_all.5.values_ref, s32[128,128]{1,0:T(8,128)S(1)} %bitcast.7), custom_call_target="tpu_custom_call" | custom-call | tf_op jit(solution)/shard_map/owner/pallas_call | solution.py:441
  (1 shorter events, 0.0 us)
Async XLA Ops:
  1.7 6.4 %collective-permute-start = (f32[24,128]{1,0:T(8,128)S(1)}, f32[24,128]{1,0:T(8,128)S(1)}, u32[]{:S(2)}, u32[]{:S(2)}) collective-permute-start(f32[24,128]{1,0:T(8,128)S(1)} %get-tuple-element.12), channel_id=1, source_target_pairs={{0,112},{16,0},{32,16},{48,32},{64,48},{80,64},{96,80},{112,96},{1... | collective-permute-start | bytes 36872 | tf_op jit(solution)/shard_map/ppermute | solution.py:374
  7.3 4.7 %collective-permute-start.1 = (f32[24,128]{1,0:T(8,128)S(1)}, f32[24,128]{1,0:T(8,128)S(1)}, u32[]{:S(2)}, u32[]{:S(2)}) collective-permute-start(f32[24,128]{1,0:T(8,128)S(1)} %get-tuple-element.13), channel_id=1, source_target_pairs={{0,16},{16,32},{32,48},{48,64},{64,80},{80,96},{96,112},{112,0},{1... | collective-permute-start | bytes 36872 | tf_op jit(solution)/shard_map/ppermute | solution.py:374
  12.0 7.7 %collective-permute-start.2 = (f32[100,256]{1,0:T(8,128)S(1)}, f32[100,256]{1,0:T(8,128)S(1)}, u32[]{:S(2)}, u32[]{:S(2)}) collective-permute-start(f32[100,256]{1,0:T(8,128)S(1)} %get-tuple-element.14), channel_id=1, source_target_pairs={{0,1},{1,0},{2,3},{3,2},{4,5},{5,4},{6,7},{7,6},{8,9},{9,8},{10,11... | collective-permute-start | bytes 307208 | tf_op jit(solution)/shard_map/ppermute | solution.py:380
  14.2 6.7 %collective-permute-start.3 = (f32[100,256]{1,0:T(8,128)S(1)}, f32[100,256]{1,0:T(8,128)S(1)}, u32[]{:S(2)}, u32[]{:S(2)}) collective-permute-start(f32[100,256]{1,0:T(8,128)S(1)} %get-tuple-element.15), channel_id=1, source_target_pairs={{0,15},{1,2},{2,1},{3,4},{4,3},{5,6},{6,5},{7,8},{8,7},{9,10},{10,... | collective-permute-start | bytes 307208 | tf_op jit(solution)/shard_map/ppermute | solution.py:380
  16.6 34.9 %copy-start = (s32[1,128,128]{2,1,0:T(8,128)S(1)}, s32[1,128,128]{2,1,0:T(8,128)}, u32[]{:S(2)}) copy-start(s32[1,128,128]{2,1,0:T(8,128)} %param.13) | copy-start | bytes 196612

commit v5 on v4

--- a/solution.py
+++ b/solution.py
@@ -20,6 +20,7 @@
 ROWS = 48
 WIDE = 3
 TABLE = LAYERS * CY * 2
+MOST = 40
 TURN = 16
 LOOKED_UP = 5
 BANDS = 6
@@ -257,7 +258,6 @@
         fetch.wait()
     counts = counts_ref[...]
     rows_used = jnp.max(jnp.sum(counts.astype(F32), axis=0, keepdims=True)).astype(jnp.int32)
-    groups = (rows_used + (8 * TURN - 1)) // (8 * TURN)
     split = split_ref[...]
     lane_id = iota((LANES, LANES), 0).astype(BF16)
     sub_id = iota((8, LANES), 0)
@@ -298,15 +298,23 @@
             found = jnp.where((rows_at >> 3) == q, value, found)
         first_ref[o] = found
 
-    def some(i, _):
-        first = i * TURN
-        for j in range(TURN - LOOKED_UP):
+    def lookup(first, size, singles):
+        for j in range(size - singles):
             by_matmul(first + j)
-        for j in range(TURN - LOOKED_UP, TURN):
+        for j in range(size - singles, size):
             by_lanes(first + j)
+
+    def most(i, _):
+        lookup(i * MOST, MOST, 13)
         return 0
 
-    lax.fori_loop(0, groups, some, 0)
+    def rest(i, _):
+        lookup(2 * MOST + i * TURN, TURN, LOOKED_UP)
+        return 0
+
+    lax.fori_loop(0, jnp.minimum((rows_used + (8 * MOST - 1)) // (8 * MOST), 2), most, 0)
+    left = jnp.maximum(rows_used - 16 * MOST, 0)
+    lax.fori_loop(0, (left + (8 * TURN - 1)) // (8 * TURN), rest, 0)
 
     old_ref, new_ref = first_ref, second_ref
     for bit in reversed(range(STAGES)):

time: 53.6 us -> 53.1 us (level)
  Pallas kernels: 20.3 us -> 19.7 us
    pallas_call x1, Pallas kernels: 14.2 us -> 13.7 us  [local(): pl.pallas_call(main_kernel, in_specs=[VMEM] * 7 + [pl.BlockSpec(memory_sp...]
where the time goes in v5:
time: 53.1 us; the launch traced here: 52.9 us
  Pallas kernels  19.7 us (37%)
  blocking collectives  16.4 us (31%)
  starting transfers between devices  10.2 us (19%)
  waiting for transfers between devices  5.92 us (11%)
  between operations  0.67 us (1%)
    all_to_all x1, blocking collectives, local(): lax.all_to_all(partial_value, ('gx', 'gy'), split_axis=0, concat_axis=0,...  16.4 us
    pallas_call x1, Pallas kernels, local(): pl.pallas_call(main_kernel, in_specs=[VMEM] * 7 + [pl.BlockSpec(memory_sp...  13.7 us
    ppermute x2, starting transfers between devices, shift(): lax.ppermute(array, axis, [(i, (i + step) % size) for i in range(size)])  5.59 us
    ppermute x2, waiting for transfers between devices, shift(): lax.ppermute(array, axis, [(i, (i + step) % size) for i in range(size)])  4.65 us
    ppermute x2, starting transfers between devices, pairs(): return lax.ppermute(array, axis, [(i, j % size) for i, j in swaps])  4.62 us
    pallas_call x1, Pallas kernels, local(): pl.pallas_call(plan_kernel, in_specs=[VMEM] * 2, out_specs=(VMEM,) * 2, o...  3.02 us
    pallas_call x1, Pallas kernels, local(): pl.pallas_call(owner_kernel, in_specs=[VMEM] * 2, out_specs=VMEM, out_sha...  1.9 us
    ppermute x2, waiting for transfers between devices, pairs(): return lax.ppermute(array, axis, [(i, j % size) for i, j in swaps])  1.27 us
  transfers between devices with their start and end apart: 4, of which 3 were waited for; matrix products, arithmetic and copies ran while one was open for 0% of the time, Pallas kernels for 6%

profile of v5, /device:TPU:1, one launch (start us, length us, event | category | flops | bytes accessed | tf_op | source)
XLA Modules:
  0.0 52.9 jit_solution(12072899824563108044)
XLA Ops:
  0.6 1.1 %pack.1 = (f32[9,24,256]{2,1,0:T(8,128)S(1)}, f32[24,128]{1,0:T(8,128)S(1)}, f32[24,128]{1,0:T(8,128)S(1)}) custom-call(f32[6,24,256]{2,1,0:T(8,128)} %bitcast.12, f32[3,24,256]{2,1,0:T(8,128)} %dif_ref.1, s32[24,256]{1,0:T(8,128)} %mask_ref.1), custom_call_target="tpu_custom_call" | custom-call | tf_op jit(solution)/shard_map/pack/pallas_call | solution.py:398
  1.7 5.6 %collective-permute-start = (f32[24,128]{1,0:T(8,128)S(1)}, f32[24,128]{1,0:T(8,128)S(1)}, u32[]{:S(2)}, u32[]{:S(2)}) collective-permute-start(f32[24,128]{1,0:T(8,128)S(1)} %get-tuple-element.12), channel_id=1, source_target_pairs={{0,112},{16,0},{32,16},{48,32},{64,48},{80,64},{96,80},{112,96},{1... | collective-permute-start | bytes 36872 | tf_op jit(solution)/shard_map/ppermute | solution.py:382
  7.3 0.0 collective-permute-start.1
  7.3 0.8 %collective-permute-done.east_ref = f32[24,128]{1,0:T(8,128)S(1)} collective-permute-done((f32[24,128]{1,0:T(8,128)S(1)}, f32[24,128]{1,0:T(8,128)S(1)}, u32[]{:S(2)}, u32[]{:S(2)}) %collective-permute-start) | collective-permute-done | bytes 12320 | tf_op jit(solution)/shard_map/ppermute | solution.py:382
  8.1 3.8 %collective-permute-done.1.west_ref = f32[24,128]{1,0:T(8,128)S(1)} collective-permute-done((f32[24,128]{1,0:T(8,128)S(1)}, f32[24,128]{1,0:T(8,128)S(1)}, u32[]{:S(2)}, u32[]{:S(2)}) %collective-permute-start.1) | collective-permute-done | bytes 12320 | tf_op jit(solution)/shard_map/ppermute | solution.py:382
  12.0 2.2 %collective-permute-start.2 = (f32[100,256]{1,0:T(8,128)S(1)}, f32[100,256]{1,0:T(8,128)S(1)}, u32[]{:S(2)}, u32[]{:S(2)}) collective-permute-start(f32[100,256]{1,0:T(8,128)S(1)} %get-tuple-element.14), channel_id=1, source_target_pairs={{0,1},{1,0},{2,3},{3,2},{4,5},{5,4},{6,7},{7,6},{8,9},{9,8},{10,11... | collective-permute-start | bytes 307208 | tf_op jit(solution)/shard_map/ppermute | solution.py:388
  14.2 2.4 %collective-permute-start.3 = (f32[100,256]{1,0:T(8,128)S(1)}, f32[100,256]{1,0:T(8,128)S(1)}, u32[]{:S(2)}, u32[]{:S(2)}) collective-permute-start(f32[100,256]{1,0:T(8,128)S(1)} %get-tuple-element.15), channel_id=1, source_target_pairs={{0,15},{1,2},{2,1},{3,4},{4,3},{5,6},{6,5},{7,8},{8,7},{9,10},{10,... | collective-permute-start | bytes 307208 | tf_op jit(solution)/shard_map/ppermute | solution.py:388
  16.6 0.0 copy-start
  16.6 3.0 %plan.1 = (s32[128,8,128]{2,1,0:T(8,128)S(1)}, s32[128,8,128]{2,1,0:T(8,128)S(1)}) custom-call(s32[128,3,8,128]{3,2,1,0:T(8,128)} %bitcast.8, s32[128,128]{1,0:T(8,128)} %bitcast.10), custom_call_target="tpu_custom_call" | custom-call | tf_op jit(solution)/shard_map/plan/pallas_call | solution.py:417
  19.6 0.0 collective-permute-done.2.one_ref
  19.6 1.3 %collective-permute-done.3.two_ref = f32[100,256]{1,0:T(8,128)S(1)} collective-permute-done((f32[100,256]{1,0:T(8,128)S(1)}, f32[100,256]{1,0:T(8,128)S(1)}, u32[]{:S(2)}, u32[]{:S(2)}) %collective-permute-start.3) | collective-permute-done | bytes 102432 | tf_op jit(solution)/shard_map/ppermute | solution.py:388
  20.9 13.7 %main.1 = (f32[6,24,256]{2,1,0:T(8,128)}, f32[128,1,128]{2,1,0:T(1,128)S(1)}) custom-call(f32[9,24,256]{2,1,0:T(8,128)S(1)} %get-tuple-element.11.base_ref, f32[24,128]{1,0:T(8,128)S(1)} %collective-permute-done.east_ref, f32[24,128]{1,0:T(8,128)S(1)} %collective-permute-done.1.west_ref, f32[100,256]{1,0:T(8,128)S(1)} %collective-permute-done.2.one_ref, ...), custom_call_target="tpu_custom_call" | custom-call | tf_op jit(solution)/shard_map/main/pallas_call | solution.py:425
  34.6 16.4 %all_to_all.5.values_ref = f32[128,1,128]{2,1,0:T(1,128)S(1)} all-to-all(f32[128,1,128]{2,1,0:T(1,128)S(1)} %get-tuple-element.19), channel_id=1, replica_groups=mesh['gx'=8,'gy'=16] {'gx','gy'}, dimensions={0} | all-to-all | bytes 131072 | tf_op jit(solution)/shard_map/all_to_all | solution.py:446
  51.0 0.0 copy-done
  51.0 1.9 %owner.1 = f32[32,128]{1,0:T(8,128)} custom-call(f32[128,1,128]{2,1,0:T(1,128)S(1)} %all_to_all.5.values_ref, s32[128,128]{1,0:T(8,128)S(1)} %bitcast.7), custom_call_target="tpu_custom_call" | custom-call | tf_op jit(solution)/shard_map/owner/pallas_call | solution.py:449
  (1 shorter events, 0.0 us)
Async XLA Ops:
  1.7 6.4 %collective-permute-start = (f32[24,128]{1,0:T(8,128)S(1)}, f32[24,128]{1,0:T(8,128)S(1)}, u32[]{:S(2)}, u32[]{:S(2)}) collective-permute-start(f32[24,128]{1,0:T(8,128)S(1)} %get-tuple-element.12), channel_id=1, source_target_pairs={{0,112},{16,0},{32,16},{48,32},{64,48},{80,64},{96,80},{112,96},{1... | collective-permute-start | bytes 36872 | tf_op jit(solution)/shard_map/ppermute | solution.py:382
  7.3 4.7 %collective-permute-start.1 = (f32[24,128]{1,0:T(8,128)S(1)}, f32[24,128]{1,0:T(8,128)S(1)}, u32[]{:S(2)}, u32[]{:S(2)}) collective-permute-start(f32[24,128]{1,0:T(8,128)S(1)} %get-tuple-element.13), channel_id=1, source_target_pairs={{0,16},{16,32},{32,48},{48,64},{64,80},{80,96},{96,112},{112,0},{1... | collective-permute-start | bytes 36872 | tf_op jit(solution)/shard_map/ppermute | solution.py:382
  12.0 7.7 %collective-permute-start.2 = (f32[100,256]{1,0:T(8,128)S(1)}, f32[100,256]{1,0:T(8,128)S(1)}, u32[]{:S(2)}, u32[]{:S(2)}) collective-permute-start(f32[100,256]{1,0:T(8,128)S(1)} %get-tuple-element.14), channel_id=1, source_target_pairs={{0,1},{1,0},{2,3},{3,2},{4,5},{5,4},{6,7},{7,6},{8,9},{9,8},{10,11... | collective-permute-start | bytes 307208 | tf_op jit(solution)/shard_map/ppermute | solution.py:388
  14.2 6.7 %collective-permute-start.3 = (f32[100,256]{1,0:T(8,128)S(1)}, f32[100,256]{1,0:T(8,128)S(1)}, u32[]{:S(2)}, u32[]{:S(2)}) collective-permute-start(f32[100,256]{1,0:T(8,128)S(1)} %get-tuple-element.15), channel_id=1, source_target_pairs={{0,15},{1,2},{2,1},{3,4},{4,3},{5,6},{6,5},{7,8},{8,7},{9,10},{10,... | collective-permute-start | bytes 307208 | tf_op jit(solution)/shard_map/ppermute | solution.py:388
  16.6 34.4 %copy-start = (s32[1,128,128]{2,1,0:T(8,128)S(1)}, s32[1,128,128]{2,1,0:T(8,128)}, u32[]{:S(2)}) copy-start(s32[1,128,128]{2,1,0:T(8,128)} %param.13) | copy-start | bytes 196612

commit v6 on v5

--- a/solution.py
+++ b/solution.py
@@ -66,13 +66,13 @@
 
     @pl.when(even)
     def _():
+        fill(one_ref, 0)
+        fill(two_ref, CY - HALO)
+
+    @pl.when(jnp.logical_not(even))
+    def _():
         fill(one_ref, CY - HALO)
         fill(two_ref, 0)
-
-    @pl.when(jnp.logical_not(even))
-    def _():
-        fill(one_ref, 0)
-        fill(two_ref, CY - HALO)
 
 
 def plan_kernel(cells_ref, counts_ref, spots_ref, moves_ref, first_ref, second_ref, shift_ref):
@@ -239,10 +239,10 @@
     place = lax.axis_index("gy")
     even = place % 2 == 0
     edge = (place == 0) | (place == lax.axis_size("gy") - 1)
-    one = one_ref[...]
-    two = jnp.where(edge, 0.0, two_ref[...])
-    north_ref[...] = jnp.where(even, one, two)
-    south_ref[...] = jnp.where(even, two, one)
+    one = jnp.where(edge, 0.0, one_ref[...])
+    two = two_ref[...]
+    north_ref[...] = jnp.where(even, two, one)
+    south_ref[...] = jnp.where(even, one, two)
     smooth(
         base_ref, east_ref, west_ref, north_ref, south_ref, smooth_ref, wide_ref, coeff_ref,
         table_ref,
@@ -411,8 +411,8 @@
         out_shape=(pltpu.VMEM(STRIP, F32),) * 2,
         name="rows",
     )(*near(base, east, west))
-    one = pairs(one, "gy", 0)
-    two = pairs(two, "gy", 1)
+    one = pairs(one, "gy", 1)
+    two = pairs(two, "gy", 0)
     whole = pltpu.VMEM((OWNERS, 8, LANES), jnp.int32)
     spots, moves = pl.pallas_call(
         plan_kernel,

time: 53.1 us -> 51.1 us (0.962)
  blocking collectives: 16.4 us -> 14.9 us
  waiting for transfers between devices: 5.92 us -> 4.66 us
  starting transfers between devices: 10.2 us -> 11 us
    all_to_all x1, blocking collectives: 16.4 us -> 14.9 us  [local(): lax.all_to_all(partial_value, ('gx', 'gy'), split_axis=0, concat_axis=0,...]
    ppermute x2, waiting for transfers between devices: 1.27 us -> 0.01 us  [pairs(): return lax.ppermute(array, axis, [(i, j % size) for i, j in swaps])]
    ppermute x2, starting transfers between devices: 4.62 us -> 5.37 us  [pairs(): return lax.ppermute(array, axis, [(i, j % size) for i, j in swaps])]
  transfers between devices with their start and end apart: 4 -> 4, of which waited for: 3 -> 2; matrix products, arithmetic and copies ran while one was open for 0% -> 0% of each run, Pallas kernels for 6% -> 6%
where the time goes in v6:
time: 51.1 us; the launch traced here: 50.9 us
  Pallas kernels  19.7 us (39%)
  blocking collectives  14.9 us (29%)
  starting transfers between devices  11 us (22%)
  waiting for transfers between devices  4.66 us (9%)
  between operations  0.68 us (1%)
    all_to_all x1, blocking collectives, local(): lax.all_to_all(partial_value, ('gx', 'gy'), split_axis=0, concat_axis=0,...  14.9 us
    pallas_call x1, Pallas kernels, local(): pl.pallas_call(main_kernel, in_specs=[VMEM] * 7 + [pl.BlockSpec(memory_sp...  13.7 us
    ppermute x2, starting transfers between devices, shift(): lax.ppermute(array, axis, [(i, (i + step) % size) for i in range(size)])  5.59 us
    ppermute x2, starting transfers between devices, pairs(): return lax.ppermute(array, axis, [(i, j % size) for i, j in swaps])  5.37 us
    ppermute x2, waiting for transfers between devices, shift(): lax.ppermute(array, axis, [(i, (i + step) % size) for i in range(size)])  4.65 us
    pallas_call x1, Pallas kernels, local(): pl.pallas_call(plan_kernel, in_specs=[VMEM] * 2, out_specs=(VMEM,) * 2, o...  3.02 us
    pallas_call x1, Pallas kernels, local(): pl.pallas_call(owner_kernel, in_specs=[VMEM] * 2, out_specs=VMEM, out_sha...  1.9 us
    pallas_call x1, Pallas kernels, local(): pl.pallas_call(pack_kernel, in_specs=[VMEM] * 3, out_specs=(VMEM,) * 3, o...  1.07 us
  transfers between devices with their start and end apart: 4, of which 2 were waited for; matrix products, arithmetic and copies ran while one was open for 0% of the time, Pallas kernels for 6%

profile of v6, /device:TPU:1, one launch (start us, length us, event | category | flops | bytes accessed | tf_op | source)
XLA Modules:
  0.0 50.9 jit_solution(5632375842766184268)
XLA Ops:
  0.6 1.1 %pack.1 = (f32[9,24,256]{2,1,0:T(8,128)S(1)}, f32[24,128]{1,0:T(8,128)S(1)}, f32[24,128]{1,0:T(8,128)S(1)}) custom-call(f32[6,24,256]{2,1,0:T(8,128)} %bitcast.12, f32[3,24,256]{2,1,0:T(8,128)} %dif_ref.1, s32[24,256]{1,0:T(8,128)} %mask_ref.1), custom_call_target="tpu_custom_call" | custom-call | tf_op jit(solution)/shard_map/pack/pallas_call | solution.py:398
  1.7 5.6 %collective-permute-start = (f32[24,128]{1,0:T(8,128)S(1)}, f32[24,128]{1,0:T(8,128)S(1)}, u32[]{:S(2)}, u32[]{:S(2)}) collective-permute-start(f32[24,128]{1,0:T(8,128)S(1)} %get-tuple-element.12), channel_id=1, source_target_pairs={{0,112},{16,0},{32,16},{48,32},{64,48},{80,64},{96,80},{112,96},{1... | collective-permute-start | bytes 36872 | tf_op jit(solution)/shard_map/ppermute | solution.py:382
  7.3 0.0 collective-permute-start.1
  7.3 0.8 %collective-permute-done.east_ref = f32[24,128]{1,0:T(8,128)S(1)} collective-permute-done((f32[24,128]{1,0:T(8,128)S(1)}, f32[24,128]{1,0:T(8,128)S(1)}, u32[]{:S(2)}, u32[]{:S(2)}) %collective-permute-start) | collective-permute-done | bytes 12320 | tf_op jit(solution)/shard_map/ppermute | solution.py:382
  8.1 3.8 %collective-permute-done.1.west_ref = f32[24,128]{1,0:T(8,128)S(1)} collective-permute-done((f32[24,128]{1,0:T(8,128)S(1)}, f32[24,128]{1,0:T(8,128)S(1)}, u32[]{:S(2)}, u32[]{:S(2)}) %collective-permute-start.1) | collective-permute-done | bytes 12320 | tf_op jit(solution)/shard_map/ppermute | solution.py:382
  12.0 4.5 %collective-permute-start.2 = (f32[100,256]{1,0:T(8,128)S(1)}, f32[100,256]{1,0:T(8,128)S(1)}, u32[]{:S(2)}, u32[]{:S(2)}) collective-permute-start(f32[100,256]{1,0:T(8,128)S(1)} %get-tuple-element.14), channel_id=1, source_target_pairs={{0,15},{1,2},{2,1},{3,4},{4,3},{5,6},{6,5},{7,8},{8,7},{9,10},{10,... | collective-permute-start | bytes 307208 | tf_op jit(solution)/shard_map/ppermute | solution.py:388
  16.5 0.9 %collective-permute-start.3 = (f32[100,256]{1,0:T(8,128)S(1)}, f32[100,256]{1,0:T(8,128)S(1)}, u32[]{:S(2)}, u32[]{:S(2)}) collective-permute-start(f32[100,256]{1,0:T(8,128)S(1)} %get-tuple-element.15), channel_id=1, source_target_pairs={{0,1},{1,0},{2,3},{3,2},{4,5},{5,4},{6,7},{7,6},{8,9},{9,8},{10,11... | collective-permute-start | bytes 307208 | tf_op jit(solution)/shard_map/ppermute | solution.py:388
  17.4 0.0 copy-start
  17.4 3.0 %plan.1 = (s32[128,8,128]{2,1,0:T(8,128)S(1)}, s32[128,8,128]{2,1,0:T(8,128)S(1)}) custom-call(s32[128,3,8,128]{3,2,1,0:T(8,128)} %bitcast.8, s32[128,128]{1,0:T(8,128)} %bitcast.10), custom_call_target="tpu_custom_call" | custom-call | tf_op jit(solution)/shard_map/plan/pallas_call | solution.py:417
  20.4 0.0 collective-permute-done.2.one_ref
  20.4 0.0 collective-permute-done.3.two_ref
  20.4 13.7 %main.1 = (f32[6,24,256]{2,1,0:T(8,128)}, f32[128,1,128]{2,1,0:T(1,128)S(1)}) custom-call(f32[9,24,256]{2,1,0:T(8,128)S(1)} %get-tuple-element.11.base_ref, f32[24,128]{1,0:T(8,128)S(1)} %collective-permute-done.east_ref, f32[24,128]{1,0:T(8,128)S(1)} %collective-permute-done.1.west_ref, f32[100,256]{1,0:T(8,128)S(1)} %collective-permute-done.2.one_ref, ...), custom_call_target="tpu_custom_call" | custom-call | tf_op jit(solution)/shard_map/main/pallas_call | solution.py:425
  34.1 14.9 %all_to_all.5.values_ref = f32[128,1,128]{2,1,0:T(1,128)S(1)} all-to-all(f32[128,1,128]{2,1,0:T(1,128)S(1)} %get-tuple-element.19), channel_id=1, replica_groups=mesh['gx'=8,'gy'=16] {'gx','gy'}, dimensions={0} | all-to-all | bytes 131072 | tf_op jit(solution)/shard_map/all_to_all | solution.py:446
  49.0 0.0 copy-done
  49.0 1.9 %owner.1 = f32[32,128]{1,0:T(8,128)} custom-call(f32[128,1,128]{2,1,0:T(1,128)S(1)} %all_to_all.5.values_ref, s32[128,128]{1,0:T(8,128)S(1)} %bitcast.7), custom_call_target="tpu_custom_call" | custom-call | tf_op jit(solution)/shard_map/owner/pallas_call | solution.py:449
  (1 shorter events, 0.0 us)
Async XLA Ops:
  1.7 6.4 %collective-permute-start = (f32[24,128]{1,0:T(8,128)S(1)}, f32[24,128]{1,0:T(8,128)S(1)}, u32[]{:S(2)}, u32[]{:S(2)}) collective-permute-start(f32[24,128]{1,0:T(8,128)S(1)} %get-tuple-element.12), channel_id=1, source_target_pairs={{0,112},{16,0},{32,16},{48,32},{64,48},{80,64},{96,80},{112,96},{1... | collective-permute-start | bytes 36872 | tf_op jit(solution)/shard_map/ppermute | solution.py:382
  7.3 4.7 %collective-permute-start.1 = (f32[24,128]{1,0:T(8,128)S(1)}, f32[24,128]{1,0:T(8,128)S(1)}, u32[]{:S(2)}, u32[]{:S(2)}) collective-permute-start(f32[24,128]{1,0:T(8,128)S(1)} %get-tuple-element.13), channel_id=1, source_target_pairs={{0,16},{16,32},{32,48},{48,64},{64,80},{80,96},{96,112},{112,0},{1... | collective-permute-start | bytes 36872 | tf_op jit(solution)/shard_map/ppermute | solution.py:382
  12.0 8.4 %collective-permute-start.2 = (f32[100,256]{1,0:T(8,128)S(1)}, f32[100,256]{1,0:T(8,128)S(1)}, u32[]{:S(2)}, u32[]{:S(2)}) collective-permute-start(f32[100,256]{1,0:T(8,128)S(1)} %get-tuple-element.14), channel_id=1, source_target_pairs={{0,15},{1,2},{2,1},{3,4},{4,3},{5,6},{6,5},{7,8},{8,7},{9,10},{10,... | collective-permute-start | bytes 307208 | tf_op jit(solution)/shard_map/ppermute | solution.py:388
  16.5 3.9 %collective-permute-start.3 = (f32[100,256]{1,0:T(8,128)S(1)}, f32[100,256]{1,0:T(8,128)S(1)}, u32[]{:S(2)}, u32[]{:S(2)}) collective-permute-start(f32[100,256]{1,0:T(8,128)S(1)} %get-tuple-element.15), channel_id=1, source_target_pairs={{0,1},{1,0},{2,3},{3,2},{4,5},{5,4},{6,7},{7,6},{8,9},{9,8},{10,11... | collective-permute-start | bytes 307208 | tf_op jit(solution)/shard_map/ppermute | solution.py:388
  17.4 31.6 %copy-start = (s32[1,128,128]{2,1,0:T(8,128)S(1)}, s32[1,128,128]{2,1,0:T(8,128)}, u32[]{:S(2)}) copy-start(s32[1,128,128]{2,1,0:T(8,128)} %param.13) | copy-start | bytes 196612

commit v7 on v6

--- a/solution.py
+++ b/solution.py
@@ -35,7 +35,7 @@
     return lax.broadcasted_iota(jnp.int32, shape, dim)
 
 
-def pack_kernel(inc_ref, dif_ref, mask_ref, base_ref, first_ref, last_ref):
+def pack_kernel(inc_ref, dif_ref, mask_ref, base_ref, far_ref, close_ref):
     wet = mask_ref[...].astype(F32)
     lane = iota((CY, LANES), 1)
     first = jnp.zeros((CY, LANES), F32)
@@ -51,11 +51,15 @@
         right = pltpu.roll(right, STRIDE * a + HALO, 1)
         first = jnp.where(mine, left, first)
         last = jnp.where(mine, right, last)
-    first_ref[...] = first
-    last_ref[...] = last
-
-
-def rows_kernel(base_ref, east_ref, west_ref, one_ref, two_ref):
+    even = lax.axis_index("gx") % 2 == 0
+    far_ref[...] = jnp.where(even, first, last)
+    close_ref[...] = jnp.where(even, last, first)
+
+
+def rows_kernel(base_ref, far_ref, close_ref, one_ref, two_ref, east_ref, west_ref):
+    even_x = lax.axis_index("gx") % 2 == 0
+    east_ref[...] = jnp.where(even_x, close_ref[...], far_ref[...])
+    west_ref[...] = jnp.where(even_x, far_ref[...], close_ref[...])
     even = lax.axis_index("gy") % 2 == 0
 
     def fill(ref, start):
@@ -377,11 +381,6 @@
     return jax.ShapeDtypeStruct(dims, F32)
 
 
-def shift(array, axis, step):
-    size = lax.axis_size(axis)
-    return lax.ppermute(array, axis, [(i, (i + step) % size) for i in range(size)])
-
-
 def pairs(array, axis, odd):
     size = lax.axis_size(axis)
     swaps = [(i, (((i + odd) % size) ^ 1) - odd) for i in range(size)]
@@ -395,22 +394,22 @@
 def local(
     increments, diffusivity, sea_mask, source_cells, source_weights, source_counts, slot_owner
 ):
-    base, first, last = pl.pallas_call(
+    base, far, close = pl.pallas_call(
         pack_kernel,
         in_specs=[VMEM] * 3,
         out_specs=(VMEM,) * 3,
         out_shape=(pltpu.VMEM((ARRAYS, CY, CX), F32),) + (pltpu.VMEM((CY, LANES), F32),) * 2,
         name="pack",
     )(increments.reshape(LAYERS, CY, CX), diffusivity, sea_mask)
-    east = shift(first, "gx", -1)
-    west = shift(last, "gx", 1)
-    one, two = pl.pallas_call(
+    far = pairs(far, "gx", 1)
+    close = pairs(close, "gx", 0)
+    one, two, east, west = pl.pallas_call(
         rows_kernel,
         in_specs=[VMEM] * 3,
-        out_specs=(VMEM,) * 2,
-        out_shape=(pltpu.VMEM(STRIP, F32),) * 2,
+        out_specs=(VMEM,) * 4,
+        out_shape=(pltpu.VMEM(STRIP, F32),) * 2 + (pltpu.VMEM((CY, LANES), F32),) * 2,
         name="rows",
-    )(*near(base, east, west))
+    )(*near(base, far, close))
     one = pairs(one, "gy", 1)
     two = pairs(two, "gy", 0)
     whole = pltpu.VMEM((OWNERS, 8, LANES), jnp.int32)

time: 51.1 us -> 49.8 us (0.975)
  waiting for transfers between devices: 4.66 us -> 2.55 us
  blocking collectives: 14.9 us -> 15.7 us
    ppermute x2 -> x4, starting transfers between devices: 5.37 us -> 11 us  [pairs(): return lax.ppermute(array, axis, [(i, j % size) for i, j in swaps])]
    ppermute x2 -> x0, starting transfers between devices: 5.59 us -> none  [shift(): lax.ppermute(array, axis, [(i, (i + step) % size) for i in range(size)])]
    ppermute x2 -> x0, waiting for transfers between devices: 4.65 us -> none  [shift(): lax.ppermute(array, axis, [(i, (i + step) % size) for i in range(size)])]
    ppermute x2 -> x4, waiting for transfers between devices: 0.01 us -> 2.55 us  [pairs(): return lax.ppermute(array, axis, [(i, j % size) for i, j in swaps])]
    all_to_all x1, blocking collectives: 14.9 us -> 15.7 us  [local(): lax.all_to_all(partial_value, ('gx', 'gy'), split_axis=0, concat_axis=0,...]
where the time goes in v7:
time: 49.8 us; the launch traced here: 49.6 us
  Pallas kernels  19.7 us (40%)
  blocking collectives  15.7 us (32%)
  starting transfers between devices  11 us (22%)
  waiting for transfers between devices  2.55 us (5%)
  between operations  0.68 us (1%)
    all_to_all x1, blocking collectives, local(): lax.all_to_all(partial_value, ('gx', 'gy'), split_axis=0, concat_axis=0,...  15.7 us
    pallas_call x1, Pallas kernels, local(): pl.pallas_call(main_kernel, in_specs=[VMEM] * 7 + [pl.BlockSpec(memory_sp...  13.7 us
    ppermute x4, starting transfers between devices, pairs(): return lax.ppermute(array, axis, [(i, j % size) for i, j in swaps])  11 us
    pallas_call x1, Pallas kernels, local(): pl.pallas_call(plan_kernel, in_specs=[VMEM] * 2, out_specs=(VMEM,) * 2, o...  3.02 us
    ppermute x4, waiting for transfers between devices, pairs(): return lax.ppermute(array, axis, [(i, j % size) for i, j in swaps])  2.55 us
    pallas_call x1, Pallas kernels, local(): pl.pallas_call(owner_kernel, in_specs=[VMEM] * 2, out_specs=VMEM, out_sha...  1.9 us
    pallas_call x1, Pallas kernels, local(): pl.pallas_call(pack_kernel, in_specs=[VMEM] * 3, out_specs=(VMEM,) * 3, o...  1.07 us
  transfers between devices with their start and end apart: 4, of which 2 were waited for; matrix products, arithmetic and copies ran while one was open for 0% of the time, Pallas kernels for 6%

profile of v7, /device:TPU:1, one launch (start us, length us, event | category | flops | bytes accessed | tf_op | source)
XLA Modules:
  0.0 49.6 jit_solution(7860044056238404378)
XLA Ops:
  0.6 1.1 %pack.1 = (f32[9,24,256]{2,1,0:T(8,128)S(1)}, f32[24,128]{1,0:T(8,128)S(1)}, f32[24,128]{1,0:T(8,128)S(1)}) custom-call(f32[6,24,256]{2,1,0:T(8,128)} %bitcast.12, f32[3,24,256]{2,1,0:T(8,128)} %dif_ref.1, s32[24,256]{1,0:T(8,128)} %mask_ref.1), custom_call_target="tpu_custom_call" | custom-call | tf_op jit(solution)/shard_map/pack/pallas_call | solution.py:397
  1.7 5.6 %collective-permute-start = (f32[24,128]{1,0:T(8,128)S(1)}, f32[24,128]{1,0:T(8,128)S(1)}, u32[]{:S(2)}, u32[]{:S(2)}) collective-permute-start(f32[24,128]{1,0:T(8,128)S(1)} %get-tuple-element.14), channel_id=1, source_target_pairs={{0,112},{16,32},{32,16},{48,64},{64,48},{80,96},{96,80},{112,0},{1... | collective-permute-start | bytes 36872 | tf_op jit(solution)/shard_map/ppermute | solution.py:387
  7.3 0.0 collective-permute-start.1
  7.3 1.1 %collective-permute-done.far_ref = f32[24,128]{1,0:T(8,128)S(1)} collective-permute-done((f32[24,128]{1,0:T(8,128)S(1)}, f32[24,128]{1,0:T(8,128)S(1)}, u32[]{:S(2)}, u32[]{:S(2)}) %collective-permute-start) | collective-permute-done | bytes 12320 | tf_op jit(solution)/shard_map/ppermute | solution.py:387
  8.4 1.5 %collective-permute-done.1.close_ref = f32[24,128]{1,0:T(8,128)S(1)} collective-permute-done((f32[24,128]{1,0:T(8,128)S(1)}, f32[24,128]{1,0:T(8,128)S(1)}, u32[]{:S(2)}, u32[]{:S(2)}) %collective-permute-start.1) | collective-permute-done | bytes 12320 | tf_op jit(solution)/shard_map/ppermute | solution.py:387
  9.9 4.5 %collective-permute-start.2 = (f32[100,256]{1,0:T(8,128)S(1)}, f32[100,256]{1,0:T(8,128)S(1)}, u32[]{:S(2)}, u32[]{:S(2)}) collective-permute-start(f32[100,256]{1,0:T(8,128)S(1)} %get-tuple-element.18), channel_id=1, source_target_pairs={{0,15},{1,2},{2,1},{3,4},{4,3},{5,6},{6,5},{7,8},{8,7},{9,10},{10,... | collective-permute-start | bytes 307208 | tf_op jit(solution)/shard_map/ppermute | solution.py:387
  14.4 0.9 %collective-permute-start.3 = (f32[100,256]{1,0:T(8,128)S(1)}, f32[100,256]{1,0:T(8,128)S(1)}, u32[]{:S(2)}, u32[]{:S(2)}) collective-permute-start(f32[100,256]{1,0:T(8,128)S(1)} %get-tuple-element.19), channel_id=1, source_target_pairs={{0,1},{1,0},{2,3},{3,2},{4,5},{5,4},{6,7},{7,6},{8,9},{9,8},{10,11... | collective-permute-start | bytes 307208 | tf_op jit(solution)/shard_map/ppermute | solution.py:387
  15.3 0.0 copy-start
  15.3 3.0 %plan.1 = (s32[128,8,128]{2,1,0:T(8,128)S(1)}, s32[128,8,128]{2,1,0:T(8,128)S(1)}) custom-call(s32[128,3,8,128]{3,2,1,0:T(8,128)} %bitcast.8, s32[128,128]{1,0:T(8,128)} %bitcast.10), custom_call_target="tpu_custom_call" | custom-call | tf_op jit(solution)/shard_map/plan/pallas_call | solution.py:416
  18.3 0.0 collective-permute-done.2.one_ref
  18.3 0.0 collective-permute-done.3.two_ref
  18.3 13.7 %main.1 = (f32[6,24,256]{2,1,0:T(8,128)}, f32[128,1,128]{2,1,0:T(1,128)S(1)}) custom-call(f32[9,24,256]{2,1,0:T(8,128)S(1)} %get-tuple-element.13.base_ref, f32[24,128]{1,0:T(8,128)S(1)} %get-tuple-element.16.east_ref, f32[24,128]{1,0:T(8,128)S(1)} %get-tuple-element.17.west_ref, f32[100,256]{1,0:T(8,128)S(1)} %collective-permute-done.2.one_ref, ...), custom_call_target="tpu_custom_call" | custom-call | tf_op jit(solution)/shard_map/main/pallas_call | solution.py:424
  32.0 15.7 %all_to_all.5.values_ref = f32[128,1,128]{2,1,0:T(1,128)S(1)} all-to-all(f32[128,1,128]{2,1,0:T(1,128)S(1)} %get-tuple-element.23), channel_id=1, replica_groups=mesh['gx'=8,'gy'=16] {'gx','gy'}, dimensions={0} | all-to-all | bytes 131072 | tf_op jit(solution)/shard_map/all_to_all | solution.py:445
  47.7 0.0 copy-done
  47.7 1.9 %owner.1 = f32[32,128]{1,0:T(8,128)} custom-call(f32[128,1,128]{2,1,0:T(1,128)S(1)} %all_to_all.5.values_ref, s32[128,128]{1,0:T(8,128)S(1)} %bitcast.7), custom_call_target="tpu_custom_call" | custom-call | tf_op jit(solution)/shard_map/owner/pallas_call | solution.py:448
  (1 shorter events, 0.0 us)
Async XLA Ops:
  1.7 6.7 %collective-permute-start = (f32[24,128]{1,0:T(8,128)S(1)}, f32[24,128]{1,0:T(8,128)S(1)}, u32[]{:S(2)}, u32[]{:S(2)}) collective-permute-start(f32[24,128]{1,0:T(8,128)S(1)} %get-tuple-element.14), channel_id=1, source_target_pairs={{0,112},{16,32},{32,16},{48,64},{64,48},{80,96},{96,80},{112,0},{1... | collective-permute-start | bytes 36872 | tf_op jit(solution)/shard_map/ppermute | solution.py:387
  7.3 2.5 %collective-permute-start.1 = (f32[24,128]{1,0:T(8,128)S(1)}, f32[24,128]{1,0:T(8,128)S(1)}, u32[]{:S(2)}, u32[]{:S(2)}) collective-permute-start(f32[24,128]{1,0:T(8,128)S(1)} %get-tuple-element.15), channel_id=1, source_target_pairs={{0,16},{16,0},{32,48},{48,32},{64,80},{80,64},{96,112},{112,96},{1... | collective-permute-start | bytes 36872 | tf_op jit(solution)/shard_map/ppermute | solution.py:387
  9.9 8.4 %collective-permute-start.2 = (f32[100,256]{1,0:T(8,128)S(1)}, f32[100,256]{1,0:T(8,128)S(1)}, u32[]{:S(2)}, u32[]{:S(2)}) collective-permute-start(f32[100,256]{1,0:T(8,128)S(1)} %get-tuple-element.18), channel_id=1, source_target_pairs={{0,15},{1,2},{2,1},{3,4},{4,3},{5,6},{6,5},{7,8},{8,7},{9,10},{10,... | collective-permute-start | bytes 307208 | tf_op jit(solution)/shard_map/ppermute | solution.py:387
  14.4 3.9 %collective-permute-start.3 = (f32[100,256]{1,0:T(8,128)S(1)}, f32[100,256]{1,0:T(8,128)S(1)}, u32[]{:S(2)}, u32[]{:S(2)}) collective-permute-start(f32[100,256]{1,0:T(8,128)S(1)} %get-tuple-element.19), channel_id=1, source_target_pairs={{0,1},{1,0},{2,3},{3,2},{4,5},{5,4},{6,7},{7,6},{8,9},{9,8},{10,11... | collective-permute-start | bytes 307208 | tf_op jit(solution)/shard_map/ppermute | solution.py:387
  15.3 32.5 %copy-start = (s32[1,128,128]{2,1,0:T(8,128)S(1)}, s32[1,128,128]{2,1,0:T(8,128)}, u32[]{:S(2)}) copy-start(s32[1,128,128]{2,1,0:T(8,128)} %param.13) | copy-start | bytes 196612
